TPU v7x, 256 devices: a whole 4x4x8 slice. The times are simulated.
256 devices in a mesh: dp: 64 (over y, z, core), rep: 4 (over x).
Axes of the slice: x: 4, y: 4, z: 8, core: 2. Of those that a mesh axis runs over, the one named last changes fastest.
Arguments:
- item_table: bfloat16 [32768, 512], P(('dp', 'rep')), may hold values from -6 to 6
- requests: int32 [256, 256, 2], P(('dp', 'rep')), may hold values from 0 to 127, as said below
- event_slot: int32 [131072], P(('dp', 'rep')), may hold values from 0 to 511, as said below
- lengths: int32 [256, 4], P(('dp', 'rep')), may hold values from 1 to 256, 512 in all within a row
- leaf_ids: int32 [131072, 8], P(('dp', 'rep')), may hold values from 0 to 31
- leaf_table: bfloat16 [256, 512], replicated, may hold values from -2.09375 to 2.09375
- w_in: bfloat16 [512, 2048], replicated, may hold values from -0.25 to 0.25
- w_out: bfloat16 [512, 512], replicated, may hold values from -0.25 to 0.25
- cotangent: bfloat16 [131072, 512], P(('dp', 'rep')), may hold values from -6 to 6
Outputs:
- output: bfloat16 [131072, 512], P(('dp', 'rep'))
- table_grad: float32 [32768, 512], P(('dp', 'rep'))
- leaf_grad: float32 [256, 512], replicated
- w_in_grad: float32 [512, 2048], replicated
- w_out_grad: float32 [512, 512], replicated
Inputs may be any that keep to these rules, and one draw needn't show every extreme that they name: `requests`: for each device and owner the 2 requested rows are distinct. `event_slot`: every one of a device's 512 slots is named by at least one of its events.
All inputs are finite; a program needn't handle non-finite values.
Results may differ from a plain program's by a relative error of at most 0.014.
Values may be sent and summed in bfloat16 or wider, within the bound.
A program may use at most 64 MiB of HBM per device.

v0:
```python
import jax
import jax.numpy as jnp
from jax import lax
from jax.sharding import PartitionSpec as P

HEADS = 4


epsilon = 1e-06


def normalize(values):
    center = values - jnp.mean(values, axis=-1, keepdims=True)
    spread = jnp.mean(center * center, axis=-1, keepdims=True)
    return center * lax.rsqrt(spread + epsilon)


def visible(lengths, count):
    ends = jnp.cumsum(lengths)
    places = jnp.arange(count, dtype=jnp.int32)
    segment = jnp.sum((places[:, None] >= ends[None, :]).astype(jnp.int32), axis=1)
    same = segment[:, None] == segment[None, :]
    return jnp.logical_and(same, places[None, :] <= places[:, None])


def front(rows, event_slot, lengths, leaf_ids, leaf_table, w_in):
    count = event_slot.shape[0]
    picker = (event_slot[:, None] == jnp.arange(rows.shape[0], dtype=jnp.int32)[None, :]).astype(
        jnp.bfloat16
    )
    leaves = leaf_table.shape[0] // leaf_ids.shape[1]
    onehot = (
        (leaf_ids[:, :, None] == jnp.arange(leaves, dtype=jnp.int32)[None, None, :])
        .reshape(count, -1)
        .astype(jnp.bfloat16)
    )
    inputs = (
        jnp.dot(picker, rows, preferred_element_type=jnp.float32)
        + jnp.dot(onehot, leaf_table, preferred_element_type=jnp.float32)
    ).astype(jnp.bfloat16)
    normed = normalize(inputs.astype(jnp.float32)).astype(jnp.bfloat16)
    hidden = jax.nn.silu(jnp.dot(normed, w_in, preferred_element_type=jnp.float32)).astype(
        jnp.bfloat16
    )
    width = w_in.shape[0]
    head_size = width // HEADS
    gates = hidden[:, 0:width]
    value_heads = hidden[:, width : 2 * width].reshape(count, HEADS, head_size)
    query_heads = hidden[:, 2 * width : 3 * width].reshape(count, HEADS, head_size)
    key_heads = hidden[:, 3 * width : 4 * width].reshape(count, HEADS, head_size)
    scores = jnp.einsum(
        "qhd,khd->hqk", query_heads, key_heads, preferred_element_type=jnp.float32
    ) * head_size ** (-0.5)
    allowed = visible(lengths, count)
    weights = jnp.where(allowed[None], jax.nn.silu(scores), 0.0).astype(jnp.bfloat16)
    mixed = jnp.einsum(
        "hqk,khd->qhd", weights, value_heads, preferred_element_type=jnp.float32
    ).reshape(count, width)
    gated = (normalize(mixed) * gates.astype(jnp.float32)).astype(jnp.bfloat16)
    return (inputs, gated)


def back(inputs, gated, w_out):
    return (
        jnp.dot(gated, w_out, preferred_element_type=jnp.float32) + inputs.astype(jnp.float32)
    ).astype(jnp.bfloat16)


def send_asked(wanted):
    result = lax.all_to_all(
        lax.all_to_all(wanted, "dp", split_axis=0, concat_axis=0, tiled=True),
        "rep",
        split_axis=1,
        concat_axis=1,
        tiled=True,
    )
    return result


def send_fetched(fetched):
    result = lax.all_to_all(
        lax.all_to_all(fetched, "dp", split_axis=0, concat_axis=0, tiled=True),
        "rep",
        split_axis=1,
        concat_axis=1,
        tiled=True,
    )
    return result


def send_returned(gradients):
    result = lax.all_to_all(
        lax.all_to_all(gradients, "dp", split_axis=0, concat_axis=0, tiled=True),
        "rep",
        split_axis=1,
        concat_axis=1,
        tiled=True,
    )
    return result


def on_device(
    item_table, requests, event_slot, lengths, leaf_ids, leaf_table, w_in, w_out, cotangent
):
    data_count = lax.axis_size("dp")
    replica_count = lax.axis_size("rep")
    width = item_table.shape[1]
    wanted = requests.reshape(data_count, replica_count, -1)
    asked = send_asked(wanted)
    fetched = item_table[asked]
    arrived = send_fetched(fetched).reshape(-1, width)

    def local_front(rows, table_leaf, weight_in):
        return front(rows, event_slot, lengths[0], leaf_ids, table_leaf, weight_in)

    (inputs, gated), pull_front = jax.vjp(local_front, arrived, leaf_table, w_in)
    output, pull_back = jax.vjp(back, inputs, gated, w_out)
    d_inputs, d_gated, d_out = pull_back(cotangent)
    d_rows, d_leaf, d_in = pull_front((d_inputs, d_gated))
    returned = send_returned(d_rows.reshape(data_count, replica_count, -1, width))
    leaf_sum, in_sum, out_sum = lax.psum(
        (d_leaf.astype(jnp.float32), d_in.astype(jnp.float32), d_out.astype(jnp.float32)),
        ("dp", "rep"),
    )
    table_grad = (
        jnp.zeros(item_table.shape, jnp.float32)
        .at[asked.reshape(-1)]
        .add(returned.reshape(-1, width).astype(jnp.float32))
    )
    share = 1.0 / (data_count * replica_count)
    return (output, table_grad, leaf_sum * share, in_sum * share, out_sum * share)


def solution(mesh):
    return jax.shard_map(
        on_device,
        mesh=mesh,
        in_specs=(
            P(("dp", "rep"), None),
            P(("dp", "rep"), None, None),
            P(("dp", "rep")),
            P(("dp", "rep"), None),
            P(("dp", "rep"), None),
            P(),
            P(),
            P(),
            P(("dp", "rep"), None),
        ),
        out_specs=(P(("dp", "rep"), None), P(("dp", "rep"), None), P(), P(), P()),
        check_vma=False,
    )
```

profile of v0, /device:TPU:1, one launch (start us, length us, event | category | flops | bytes accessed | tf_op | source)
XLA Modules:
  0.0 432.4 jit_solution(8049075674224172676)
XLA Ops:
  8.2 22.7 %all_to_all.30 = s32[64,4,2]{1,2,0:T(2,128)S(1)} all-to-all(s32[64,4,2]{1,2,0:T(2,128)S(1)} %copy.143), channel_id=1, replica_groups=mesh['dp'=64,'rep'=4] {'dp'}, dimensions={0} | all-to-all | bytes 4096 | tf_op jit(solution)/shard_map/all_to_all | solution.py:71
  31.1 7.9 %all_to_all.31 = s32[4,1,128]{2,1,0:T(1,128)S(1)} all-to-all(s32[4,1,128]{2,1,0:T(1,128)S(1)} %reshape.234), channel_id=1, replica_groups=mesh['dp'=64,'rep'=4] {'rep'}, dimensions={0} | all-to-all | bytes 4096 | tf_op jit(solution)/shard_map/all_to_all | solution.py:70
  40.6 2.9 gather_fusion
  44.5 6.0 %all-to-all-start.2 = ((bf16[64,4,2,512]{3,2,1,0:T(2,128)(2,1)}), bf16[64,4,2,512]{3,2,1,0:T(2,128)(2,1)S(1)}, u32[]{:S(2)}, u32[]{:S(2)}) async-start(bf16[64,4,2,512]{3,2,1,0:T(2,128)(2,1)} %reshape.215), calls=%async_computation.2 | async-start | bytes 1048576 | tf_op jit(solution)/shard_map/all_to_all | solution.py:82
  52.1 15.9 %all-to-all-done.2 = bf16[64,4,2,512]{3,2,1,0:T(2,128)(2,1)S(1)} async-done(((bf16[64,4,2,512]{3,2,1,0:T(2,128)(2,1)}), bf16[64,4,2,512]{3,2,1,0:T(2,128)(2,1)S(1)}, u32[]{:S(2)}, u32[]{:S(2)}) %all-to-all-start.2) | async-done | bytes 524320 | tf_op jit(solution)/shard_map/all_to_all | solution.py:82
  69.1 3.5 all-to-all-start.3
  73.0 2.3 fusion.42
  75.3 6.5 %all-to-all-done.3 = bf16[64,4,2,512]{3,2,0,1:T(2,128)(2,1)S(1)} async-done(((bf16[64,4,2,512]{3,2,0,1:T(2,128)(2,1)}), bf16[64,4,2,512]{3,2,0,1:T(2,128)(2,1)S(1)}, u32[]{:S(2)}, u32[]{:S(2)}) %all-to-all-start.3) | async-done | bytes 524320 | tf_op jit(solution)/shard_map/all_to_all | solution.py:81
  87.7 3.9 multiply_convert_fusion
  98.2 4.8 %select_convert_fusion = (bf16[4,512,512]{2,1,0:T(8,128)(2,1)S(1)}, f32[4,512,512]{2,1,0:T(8,128)}) fusion(pred[512,512]{1,0:T(8,128)(4,1)S(1)} %fusion.22, bf16[512,4,128]{0,2,1:T(8,128)(2,1)} %bitcast.68, bf16[512,4,128]{0,2,1:T(8,128)(2,1)} %bitcast.70), kind=kOutput, calls=%fused_computation.11 | convolution fusion | flops 275775488 | bytes 7602176 | tf_op jit(solution)/shard_map/jvp(qhd,khd->hqk)/dot_general | solution.py:51
  105.6 2.6 copy.171
  111.0 3.0 fusion.40
  117.0 5.1 %fusion.4 = bf16[4,512,512]{2,1,0:T(8,128)(2,1)S(1)} fusion(f32[4,512,512]{2,1,0:T(8,128)} %get-tuple-element.57, pred[512,512]{1,0:T(8,128)(4,1)S(1)} %fusion.22, bf16[4,128,512]{2,1,0:T(8,128)(2,1)} %bitcast.72, bf16[64,4,8,128]{3,2,1,0:T(8,128)(2,1)} %get-tuple-element.46), kind=kOutput, calls=%fused_computation.10 | convolution fusion | flops 283115520 | bytes 7602176 | tf_op jit(solution)/shard_map/transpose(jvp(hqk,khd->qhd))/dot_general | solution.py:56
  132.6 3.6 fusion
  136.2 3.3 fusion.5
  145.0 2.5 convolution_convert_fusion.1
  149.6 7.1 %all-to-all-start.4 = ((bf16[64,4,2,512]{3,2,1,0:T(2,128)(2,1)}), bf16[64,4,2,512]{3,2,1,0:T(2,128)(2,1)}, u32[]{:S(2)}, u32[]{:S(2)}) async-start(bf16[64,4,2,512]{3,2,1,0:T(2,128)(2,1)} %reshape.212), calls=%async_computation.4 | async-start | bytes 1048576 | tf_op jit(solution)/shard_map/all_to_all | solution.py:93
  157.0 19.4 %all-to-all-done.4 = bf16[64,4,2,512]{3,2,1,0:T(2,128)(2,1)} async-done(((bf16[64,4,2,512]{3,2,1,0:T(2,128)(2,1)}), bf16[64,4,2,512]{3,2,1,0:T(2,128)(2,1)}, u32[]{:S(2)}, u32[]{:S(2)}) %all-to-all-start.4) | async-done | bytes 524320 | tf_op jit(solution)/shard_map/all_to_all | solution.py:93
  178.6 4.4 %all-to-all-start.5 = ((bf16[64,4,2,512]{3,2,0,1:T(2,128)(2,1)}), bf16[64,4,2,512]{3,2,0,1:T(2,128)(2,1)}, u32[]{:S(2)}, u32[]{:S(2)}) async-start(bf16[64,4,2,512]{3,2,0,1:T(2,128)(2,1)} %copy.164), calls=%async_computation.5 | async-start | bytes 1048576 | tf_op jit(solution)/shard_map/all_to_all | solution.py:92
  183.0 2.3 fusion.11
  187.4 5.4 %all-to-all-done.5 = bf16[64,4,2,512]{3,2,0,1:T(2,128)(2,1)} async-done(((bf16[64,4,2,512]{3,2,0,1:T(2,128)(2,1)}), bf16[64,4,2,512]{3,2,0,1:T(2,128)(2,1)}, u32[]{:S(2)}, u32[]{:S(2)}) %all-to-all-start.5) | async-done | bytes 524320 | tf_op jit(solution)/shard_map/all_to_all | solution.py:92
  196.5 4.9 %scatter_custom_fusion = f32[128,512]{1,0:T(8,128)} fusion(s32[512]{0:T(512)S(1)} %bitcast.79, f32[512,512]{1,0:T(8,128)} %reshape.226, f32[]{:T(128)} %constant.15.clone.1), kind=kCustom, calls=%fused_computation.74 | custom fusion | flops 262144 | bytes 262656 | tf_op jit(solution)/shard_map/scatter-add | solution.py:128
  201.4 217.4 %all-reduce.7.cloned.1.call-done = (f32[256,512]{1,0:T(8,128)}, f32[512,2048]{1,0:T(8,128)}, f32[512,512]{1,0:T(8,128)}) async-done(((f32[256,512]{1,0:T(8,128)}, f32[512,2048]{1,0:T(8,128)}, f32[512,512]{1,0:T(8,128)}), (f32[256,512]{1,0:T(8,128)}, f32[512,2048]{1,0:T(8,128)}, f32[512,512]{1,0:T(8,128)})) %all-reduce.7.cloned.1.call-update) | async-done | bytes 5767184 | tf_op jit(solution)/shard_map/psum | solution.py:121
  418.8 4.9 %broadcast_multiply_fusion = f32[512,2048]{1,0:T(8,128)} fusion(f32[512,2048]{1,0:T(8,128)} %get-tuple-element.41), kind=kLoop, calls=%fused_computation.17 | loop fusion | flops 1048576 | bytes 8388608 | tf_op jit(solution)/shard_map/mul | solution.py:131
  (107 shorter events, 55.9 us)
Async XLA Ops:
  7.2 80.5 %copy-start = (bf16[512,2048]{1,0:T(8,128)(2,1)S(1)}, bf16[512,2048]{1,0:T(8,128)(2,1)}, u32[]{:S(2)}) copy-start(bf16[512,2048]{1,0:T(8,128)(2,1)} %param.15) | copy-start | bytes 6291460
  7.2 43.5 %copy-start.21 = (s32[1,4]{1,0:T(1,128)S(1)}, s32[1,4]{1,0:T(1,128)}, u32[]{:S(2)}) copy-start(s32[1,4]{1,0:T(1,128)} %param.12) | copy-start | bytes 52
  7.2 43.6 %copy-start.4 = (bf16[512,512]{1,0:T(8,128)(2,1)S(1)}, bf16[512,512]{1,0:T(8,128)(2,1)}, u32[]{:S(2)}) copy-start(bf16[512,512]{1,0:T(8,128)(2,1)} %param.17) | copy-start | bytes 1572868
  31.0 20.9 %copy-start.18 = (s32[512,8]{0,1:T(8,128)S(1)}, s32[512,8]{0,1:T(8,128)}, u32[]{:S(2)}) copy-start(s32[512,8]{0,1:T(8,128)} %param.13) | copy-start | bytes 49156
  44.5 40.4 %copy-start.19 = (s32[512]{0:T(512)S(1)}, s32[512]{0:T(512)}, u32[]{:S(2)}) copy-start(s32[512]{0:T(512)} %param.11) | copy-start | bytes 6148
  44.5 23.4 %all-to-all-start.2 = ((bf16[64,4,2,512]{3,2,1,0:T(2,128)(2,1)}), bf16[64,4,2,512]{3,2,1,0:T(2,128)(2,1)S(1)}, u32[]{:S(2)}, u32[]{:S(2)}) async-start(bf16[64,4,2,512]{3,2,1,0:T(2,128)(2,1)} %reshape.215), calls=%async_computation.2 | async-start | bytes 1048576 | tf_op jit(solution)/shard_map/all_to_all | solution.py:82
  69.1 12.6 %all-to-all-start.3 = ((bf16[64,4,2,512]{3,2,0,1:T(2,128)(2,1)}), bf16[64,4,2,512]{3,2,0,1:T(2,128)(2,1)S(1)}, u32[]{:S(2)}, u32[]{:S(2)}) async-start(bf16[64,4,2,512]{3,2,0,1:T(2,128)(2,1)} %copy.146), calls=%async_computation.3 | async-start | bytes 1048576 | tf_op jit(solution)/shard_map/all_to_all | solution.py:81
  72.6 346.2 %all-reduce.7.cloned.1.call-start = ((), (), s32[]{:S(2)}) async-start(), calls=%async_computation.6 | async-start | bytes 11534336 | tf_op jit(solution)/shard_map/psum | solution.py:121
  91.6 1.4 copy-start.7
  98.2 4.9 %copy-start.8 = (bf16[64,4,8,128]{3,2,1,0:T(8,128)(2,1)S(1)}, bf16[64,4,8,128]{3,2,1,0:T(8,128)(2,1)}, u32[]{:S(2)}) copy-start(bf16[64,4,8,128]{3,2,1,0:T(8,128)(2,1)} %get-tuple-element.46) | copy-start | bytes 1572868
  103.0 2.6 copy-start.2
  117.0 5.1 %copy-start.10 = (bf16[512,512]{0,1:T(8,128)(2,1)S(1)}, bf16[512,512]{0,1:T(8,128)(2,1)}, u32[]{:S(2)}) copy-start(bf16[512,512]{0,1:T(8,128)(2,1)} %copy.176) | copy-start | bytes 1572868
  117.0 6.3 %copy-start.11 = (bf16[512,512]{0,1:T(8,128)(2,1)S(1)}, bf16[512,512]{0,1:T(8,128)(2,1)}, u32[]{:S(2)}) copy-start(bf16[512,512]{0,1:T(8,128)(2,1)} %copy.177) | copy-start | bytes 1572868
  122.1 2.9 copy-start.3
  122.1 2.9 copy-start.13
  139.5 1.3 copy-start.17
  139.5 1.6 copy-start.9
  139.5 4.0 copy-start.5
  143.5 1.5 copy-start.20
  145.0 38.0 %copy-start.6 = (bf16[512,512]{1,0:T(8,128)(2,1)S(1)}, bf16[512,512]{1,0:T(8,128)(2,1)}, u32[]{:S(2)}) copy-start(bf16[512,512]{1,0:T(8,128)(2,1)} %get-tuple-element.45) | copy-start | bytes 1572868
  149.6 26.8 %all-to-all-start.4 = ((bf16[64,4,2,512]{3,2,1,0:T(2,128)(2,1)}), bf16[64,4,2,512]{3,2,1,0:T(2,128)(2,1)}, u32[]{:S(2)}, u32[]{:S(2)}) async-start(bf16[64,4,2,512]{3,2,1,0:T(2,128)(2,1)} %reshape.212), calls=%async_computation.4 | async-start | bytes 1048576 | tf_op jit(solution)/shard_map/all_to_all | solution.py:93
  178.6 14.2 %all-to-all-start.5 = ((bf16[64,4,2,512]{3,2,0,1:T(2,128)(2,1)}), bf16[64,4,2,512]{3,2,0,1:T(2,128)(2,1)}, u32[]{:S(2)}, u32[]{:S(2)}) async-start(bf16[64,4,2,512]{3,2,0,1:T(2,128)(2,1)} %copy.164), calls=%async_computation.5 | async-start | bytes 1048576 | tf_op jit(solution)/shard_map/all_to_all | solution.py:92
  418.8 4.9 %copy-start.14 = (f32[512,512]{1,0:T(8,128)S(1)}, f32[512,512]{1,0:T(8,128)}, u32[]{:S(2)}) copy-start(f32[512,512]{1,0:T(8,128)} %get-tuple-element.42) | copy-start | bytes 3145732
  418.8 6.0 %copy-start.15 = (f32[256,512]{1,0:T(8,128)S(1)}, f32[256,512]{1,0:T(8,128)}, u32[]{:S(2)}) copy-start(f32[256,512]{1,0:T(8,128)} %get-tuple-element.40) | copy-start | bytes 1572868
  (3 other events, 2.3 us)
Sparse Core Ops, SparseCore 0:
  145.1 273.6 all-reduce.6
where the time goes:
time: 434 us; the launch traced here: 432 us
  waiting for transfers between devices  264 us (61%)
  local copies, waits for them, and re-layouts  40.3 us (9%)
  matrix products  37.4 us (9%)
  blocking collectives  30.7 us (7%)
  other arithmetic  24 us (6%)
  starting transfers between devices  21.2 us (5%)
  between operations  14.4 us (3%)
    psum x1, waiting for transfers between devices, on_device(): lax.psum((d_leaf.astype(jnp.float32), d_in.astype(jnp.float32), d_out.ast...  217 us
    all_to_all x1, blocking collectives, send_asked(): lax.all_to_all(wanted, 'dp', split_axis=0, concat_axis=0, tiled=True)  22.7 us
    all_to_all x1, waiting for transfers between devices, send_returned(): lax.all_to_all(gradients, 'dp', split_axis=0, concat_axis=0, tiled=True)  19.4 us
    all_to_all x1, waiting for transfers between devices, send_fetched(): lax.all_to_all(fetched, 'dp', split_axis=0, concat_axis=0, tiled=True)  15.9 us
  transfers between devices with their start and end apart: 5, of which 5 were waited for; matrix products, arithmetic and copies ran while one was open for 6% of the time, Pallas kernels for 0%

commit v1 on v0

--- a/solution.py
+++ b/solution.py
@@ -1,6 +1,8 @@
 import jax
 import jax.numpy as jnp
 from jax import lax
+from jax.experimental import pallas as pl
+from jax.experimental.pallas import tpu as pltpu
 from jax.sharding import PartitionSpec as P
 
 HEADS = 4
@@ -99,6 +101,218 @@
     return result
 
 
+MESH = pl.DeviceIdType.MESH
+ROWS_ALL = 3072
+HALF = 1536
+R1 = 384
+R2 = 96
+RZ = 48
+
+
+def here():
+    dp = lax.axis_index("dp")
+    x = lax.axis_index("rep")
+    c = lax.rem(dp, 2)
+    z = lax.rem(dp // 2, 8)
+    y = dp // 16
+    return x, y, z, c
+
+
+def device(x, y, z, c):
+    return ((y * 8 + z) * 2 + c, x)
+
+
+def span(start, size):
+    return pl.ds(pl.multiple_of(start, size), size)
+
+
+def add_into(dst, start, sources, rows, step):
+    def body(i, carry):
+        total = None
+        for ref, first in sources:
+            part = ref[pl.ds(pl.multiple_of(first + i * step, 16), step), :].astype(jnp.float32)
+            total = part if total is None else total + part
+        dst[pl.ds(pl.multiple_of(start + i * step, 16), step), :] = total.astype(dst.dtype)
+        return carry
+
+    lax.fori_loop(0, rows // step, body, 0)
+
+
+def sum_kernel(g, out, w, r0, r1a, r1b, r2a, r2b, rz, ssem, rsem):
+    x, y, z, c = here()
+    p1 = (1 - c) * x + c * y
+    p2 = c * x + (1 - c) * y
+
+    def axis1(d):
+        return device(lax.rem(x + (1 - c) * d, 4), lax.rem(y + c * d, 4), z, c)
+
+    def axis2(d):
+        return device(lax.rem(x + c * d, 4), lax.rem(y + (1 - c) * d, 4), z, c)
+
+    def axisz(d):
+        return device(x, y, lax.rem(z + d, 8), c)
+
+    partner = device(x, y, z, 1 - c)
+    barrier = pltpu.get_barrier_semaphore()
+    peers = [partner, axis1(1), axis1(3), axis2(1), axis2(3)] + [axisz(j) for j in range(1, 8)]
+    for peer in peers:
+        pl.semaphore_signal(barrier, inc=1, device_id=peer, device_id_type=MESH)
+    pl.semaphore_wait(barrier, len(peers))
+
+    started = []
+
+    def send(src, dst, index, to):
+        copy = pltpu.make_async_remote_copy(
+            src_ref=src,
+            dst_ref=dst,
+            send_sem=ssem.at[index],
+            recv_sem=rsem.at[index],
+            device_id=to,
+            device_id_type=MESH,
+        )
+        copy.start()
+        started.append(copy)
+
+    def arrive(ref, index):
+        pltpu.make_async_remote_copy(
+            src_ref=ref,
+            dst_ref=ref,
+            send_sem=ssem.at[index],
+            recv_sem=rsem.at[index],
+            device_id=partner,
+            device_id_type=MESH,
+        ).wait_recv()
+
+    base = c * HALF
+    other = (1 - c) * HALF
+    order = (2, 1, 3, 0)
+    for k, off in enumerate(order):
+        q = lax.rem(p2 + off, 4)
+        send(g.at[span(other + q * R1, R1), :], r0.at[span(q * R1, R1), :], k, partner)
+
+    def ring_sum(pos, first, rows, right, left, ra, rb, index, local, own):
+        half = rows // 2
+        q2 = lax.rem(pos + 2, 4)
+        q1 = lax.rem(pos + 1, 4)
+        q3 = lax.rem(pos + 3, 4)
+        local(q2, 0)
+        at = first + q2 * rows
+        send(w.at[span(at, half), :], ra.at[0], index, right)
+        send(w.at[span(at + half, half), :], ra.at[1], index + 1, left)
+        local(q1, 1)
+        local(q3, 2)
+        arrive(ra.at[0], index)
+        at = first + q1 * rows
+        add_into(w, at, [(w, at), (ra.at[0], 0)], half, 48)
+        send(w.at[span(at, rows), :], rb.at[0], index + 2, right)
+        arrive(ra.at[1], index + 1)
+        at = first + q3 * rows
+        add_into(w, at + half, [(w, at + half), (ra.at[1], 0)], half, 48)
+        send(w.at[span(at, rows), :], rb.at[1], index + 3, left)
+        own()
+        arrive(rb.at[0], index + 2)
+        arrive(rb.at[1], index + 3)
+
+    def local1(q, k):
+        at = q * R1
+        arrive(r0.at[span(at, R1), :], k)
+        add_into(w, at, [(g, base + at), (r0, at)], R1, 48)
+
+    w1 = p1 * R1
+    ring_sum(
+        p1, 0, R1, axis1(1), axis1(3), r1a, r1b, 4, local1,
+        lambda: arrive(r0.at[span(w1, R1), :], 3),
+    )
+    add_into(w, w1, [(g, base + w1), (r0, w1), (r1b.at[0], 0), (r1b.at[1], 0)], R1, 48)
+    w2 = w1 + p2 * R2
+    ring_sum(
+        p2, w1, R2, axis2(1), axis2(3), r2a, r2b, 8, lambda q, k: None, lambda: None
+    )
+    add_into(w, w2, [(w, w2), (r2b.at[0], 0), (r2b.at[1], 0)], R2, 48)
+
+    def part(j):
+        return j // 4 * RZ, lax.rem(j, 4) * 128
+
+    for j in range(1, 8):
+        row, column = part(lax.rem(z + j, 8))
+        send(
+            w.at[pl.ds(pl.multiple_of(w2 + row, RZ), RZ), span(column, 128)],
+            rz.at[j - 1],
+            11 + j,
+            axisz(j),
+        )
+    row, column = part(z)
+    total = w[pl.ds(pl.multiple_of(w2 + row, RZ), RZ), span(column, 128)].astype(jnp.float32)
+    for j in range(1, 8):
+        arrive(rz.at[j - 1], 11 + j)
+        total = total + rz[j - 1].astype(jnp.float32)
+    mine = (pl.ds(pl.multiple_of(base + w2 + row, RZ), RZ), span(column, 128))
+    out[mine] = total.astype(out.dtype)
+    for j in range(1, 8):
+        send(out.at[mine], out.at[mine], 18 + j, axisz(j))
+    for j in range(1, 8):
+        row, column = part(lax.rem(z + 8 - j, 8))
+        arrive(out.at[pl.ds(pl.multiple_of(base + w2 + row, RZ), RZ), span(column, 128)], 18 + j)
+
+    def ring_share(pos, first, rows, right, left, index, ready):
+        half = rows // 2
+        at = first + pos * rows
+        send(out.at[span(at, rows), :], out.at[span(at, rows), :], index, right)
+        send(out.at[span(at, rows), :], out.at[span(at, rows), :], index + 1, left)
+        ready(pos, 0)
+        q = lax.rem(pos + 3, 4)
+        at = first + q * rows
+        arrive(out.at[span(at, rows), :], index)
+        send(out.at[span(at, half), :], out.at[span(at, half), :], index + 2, right)
+        ready(q, 1)
+        q = lax.rem(pos + 1, 4)
+        at = first + q * rows
+        arrive(out.at[span(at, rows), :], index + 1)
+        send(out.at[span(at + half, half), :], out.at[span(at + half, half), :], index + 3, left)
+        ready(q, 2)
+        q = lax.rem(pos + 2, 4)
+        at = first + q * rows
+        arrive(out.at[span(at, half), :], index + 2)
+        arrive(out.at[span(at + half, half), :], index + 3)
+        ready(q, 3)
+
+    ring_share(p2, base + w1, R2, axis2(1), axis2(3), 26, lambda q, k: None)
+
+    def pass_on(q, k):
+        rows = out.at[span(base + q * R1, R1), :]
+        send(rows, rows, 34 + k, partner)
+
+    ring_share(p1, base, R1, axis1(1), axis1(3), 30, pass_on)
+    for k, off in enumerate((0, 3, 1, 2)):
+        q = lax.rem(p2 + off, 4)
+        arrive(out.at[span(other + q * R1, R1), :], 34 + k)
+    for copy in started:
+        copy.wait_send()
+
+
+def sum_all(g):
+    vmem = pl.BlockSpec(memory_space=pltpu.VMEM)
+    bf16 = jnp.bfloat16
+    return pl.pallas_call(
+        sum_kernel,
+        out_shape=jax.ShapeDtypeStruct((ROWS_ALL, 512), bf16),
+        in_specs=[vmem],
+        out_specs=vmem,
+        scratch_shapes=[
+            pltpu.VMEM((HALF, 512), bf16),
+            pltpu.VMEM((HALF, 512), bf16),
+            pltpu.VMEM((2, R1 // 2, 512), bf16),
+            pltpu.VMEM((2, R1, 512), bf16),
+            pltpu.VMEM((2, R2 // 2, 512), bf16),
+            pltpu.VMEM((2, R2, 512), bf16),
+            pltpu.VMEM((7, RZ, 128), bf16),
+            pltpu.SemaphoreType.DMA((38,)),
+            pltpu.SemaphoreType.DMA((38,)),
+        ],
+        compiler_params=pltpu.CompilerParams(collective_id=0, has_side_effects=True),
+    )(g)
+
+
 def on_device(
     item_table, requests, event_slot, lengths, leaf_ids, leaf_table, w_in, w_out, cotangent
 ):
@@ -118,10 +332,14 @@
     d_inputs, d_gated, d_out = pull_back(cotangent)
     d_rows, d_leaf, d_in = pull_front((d_inputs, d_gated))
     returned = send_returned(d_rows.reshape(data_count, replica_count, -1, width))
-    leaf_sum, in_sum, out_sum = lax.psum(
-        (d_leaf.astype(jnp.float32), d_in.astype(jnp.float32), d_out.astype(jnp.float32)),
-        ("dp", "rep"),
-    )
+    stacked = jnp.concatenate(
+        [d_in[:, i * width : (i + 1) * width] for i in range(4)]
+        + [d_out, d_leaf, jnp.zeros((ROWS_ALL - 2816, width), jnp.bfloat16)]
+    )
+    sums = sum_all(stacked).astype(jnp.float32)
+    in_sum = jnp.concatenate([sums[i * width : (i + 1) * width] for i in range(4)], axis=1)
+    out_sum = sums[2048:2560]
+    leaf_sum = sums[2560:2816]
     table_grad = (
         jnp.zeros(item_table.shape, jnp.float32)
         .at[asked.reshape(-1)]

time: 434 us -> 247 us (0.57)
  waiting for transfers between devices: 264 us -> 21.4 us
  Pallas kernels: 0 us -> 64.8 us
  between operations: 14.4 us -> 1 us
  local copies, waits for them, and re-layouts: 40.3 us -> 46.8 us
  matrix products: 37.4 us -> 32.7 us
    psum x1 -> x0, waiting for transfers between devices: 217 us -> none  [on_device(): lax.psum((d_leaf.astype(jnp.float32), d_in.astype(jnp.float32), d_out.ast...]
    pallas_call x0 -> x1, Pallas kernels: none -> 64.8 us  [sum_all(): pl.pallas_call(sum_kernel, out_shape=jax.ShapeDtypeStruct((ROWS_ALL, 512)...]
    all_to_all x1, waiting for transfers between devices: 19.4 us -> 0.01 us  [send_returned(): lax.all_to_all(gradients, 'dp', split_axis=0, concat_axis=0, tiled=True)]
    unnamed x49 -> x45, local copies, waits for them, and re-layouts: 8.1 us -> 14 us
    all_to_all x1, waiting for transfers between devices: 5.38 us -> 0.67 us  [send_returned(): lax.all_to_all(lax.all_to_all(gradients, 'dp', split_axis=0, concat_axis=...]
  transfers between devices with their start and end apart: 5 -> 4, of which waited for: 5 -> 3; matrix products, arithmetic and copies ran while one was open for 6% -> 11% of each run, Pallas kernels for 0% -> 26%
where the time goes in v1:
time: 247 us; the launch traced here: 245 us
  Pallas kernels  64.8 us (26%)
  local copies, waits for them, and re-layouts  46.8 us (19%)
  matrix products  32.7 us (13%)
  blocking collectives  30.7 us (12%)
  other arithmetic  27.8 us (11%)
  waiting for transfers between devices  21.4 us (9%)
  starting transfers between devices  20.3 us (8%)
    pallas_call x1, Pallas kernels, sum_all(): pl.pallas_call(sum_kernel, out_shape=jax.ShapeDtypeStruct((ROWS_ALL, 512)...  64.8 us
    all_to_all x1, blocking collectives, send_asked(): lax.all_to_all(wanted, 'dp', split_axis=0, concat_axis=0, tiled=True)  22.7 us
    unnamed x45, local copies, waits for them, and re-layouts  14 us
    all_to_all x1, waiting for transfers between devices, send_fetched(): lax.all_to_all(fetched, 'dp', split_axis=0, concat_axis=0, tiled=True)  12.8 us
    all_to_all x1, waiting for transfers between devices, send_fetched(): lax.all_to_all(lax.all_to_all(fetched, 'dp', split_axis=0, concat_axis=0,...  7.94 us
    all_to_all x1, blocking collectives, send_asked(): lax.all_to_all(lax.all_to_all(wanted, 'dp', split_axis=0, concat_axis=0,...  7.92 us
    dot_general x3, matrix products, front(): jnp.einsum('qhd,khd->hqk', query_heads, key_heads, preferred_element_type...  7.66 us
    all_to_all x1, starting transfers between devices, send_returned(): lax.all_to_all(gradients, 'dp', split_axis=0, concat_axis=0, tiled=True)  6.94 us
  transfers between devices with their start and end apart: 4, of which 3 were waited for; matrix products, arithmetic and copies ran while one was open for 11% of the time, Pallas kernels for 26%

profile of v1, /device:TPU:1, one launch (start us, length us, event | category | flops | bytes accessed | tf_op | source)
XLA Modules:
  0.0 245.5 jit_solution(12872162838767427024)
XLA Ops:
  1.7 22.7 %all_to_all.30 = s32[64,4,2]{1,2,0:T(2,128)S(1)} all-to-all(s32[64,4,2]{1,2,0:T(2,128)S(1)} %copy.143), channel_id=1, replica_groups=mesh['dp'=64,'rep'=4] {'dp'}, dimensions={0} | all-to-all | bytes 4096 | tf_op jit(solution)/shard_map/all_to_all | solution.py:73
  24.6 7.9 %all_to_all.31 = s32[4,1,128]{2,1,0:T(1,128)S(1)} all-to-all(s32[4,1,128]{2,1,0:T(1,128)S(1)} %reshape.234), channel_id=1, replica_groups=mesh['dp'=64,'rep'=4] {'rep'}, dimensions={0} | all-to-all | bytes 4096 | tf_op jit(solution)/shard_map/all_to_all | solution.py:72
  34.1 2.9 %gather_fusion = bf16[512,512]{1,0:T(8,128)(2,1)S(1)} fusion(bf16[128,512]{1,0:T(8,128)(2,1)} %param.9, s32[1024]{0:T(1024)S(1)} %pad_clamp_fusion), kind=kCustom, calls=%fused_computation | custom fusion | bytes 1050624 | tf_op jit(solution)/shard_map/gather | solution.py:324
  38.0 6.0 %all-to-all-start.2 = ((bf16[64,4,2,512]{3,2,1,0:T(2,128)(2,1)}), bf16[64,4,2,512]{3,2,1,0:T(2,128)(2,1)S(1)}, u32[]{:S(2)}, u32[]{:S(2)}) async-start(bf16[64,4,2,512]{3,2,1,0:T(2,128)(2,1)} %reshape.215), calls=%async_computation.2 | async-start | bytes 1048576 | tf_op jit(solution)/shard_map/all_to_all | solution.py:84
  48.6 12.8 %all-to-all-done.2 = bf16[64,4,2,512]{3,2,1,0:T(2,128)(2,1)S(1)} async-done(((bf16[64,4,2,512]{3,2,1,0:T(2,128)(2,1)}), bf16[64,4,2,512]{3,2,1,0:T(2,128)(2,1)S(1)}, u32[]{:S(2)}, u32[]{:S(2)}) %all-to-all-start.2) | async-done | bytes 524320 | tf_op jit(solution)/shard_map/all_to_all | solution.py:84
  62.5 3.7 %all-to-all-start.3 = ((bf16[64,4,2,512]{3,2,0,1:T(2,128)(2,1)}), bf16[64,4,2,512]{3,2,0,1:T(2,128)(2,1)S(1)}, u32[]{:S(2)}, u32[]{:S(2)}) async-start(bf16[64,4,2,512]{3,2,0,1:T(2,128)(2,1)} %copy.146), calls=%async_computation.3 | async-start | bytes 1048576 | tf_op jit(solution)/shard_map/all_to_all | solution.py:83
  67.2 7.9 %all-to-all-done.3 = bf16[64,4,2,512]{3,2,0,1:T(2,128)(2,1)S(1)} async-done(((bf16[64,4,2,512]{3,2,0,1:T(2,128)(2,1)}), bf16[64,4,2,512]{3,2,0,1:T(2,128)(2,1)S(1)}, u32[]{:S(2)}, u32[]{:S(2)}) %all-to-all-start.3) | async-done | bytes 524320 | tf_op jit(solution)/shard_map/all_to_all | solution.py:83
  78.8 3.9 %multiply_convert_fusion = (bf16[512,2048]{1,0:T(8,128)(2,1)S(1)}, f32[512,2048]{1,0:T(8,128)}) fusion(bf16[512,2048]{1,0:T(8,128)(2,1)S(1)} %copy-done, bf16[512,512]{0,1:T(8,128)(2,1)S(1)} %get-tuple-element.54, f32[512]{0:T(512)S(1)} %fusion.37, f32[512]{0:T(512)S(1)} %broadcast_multiply_fusion.1), kind=kOutput, calls=%fused_computation.14 | convolution fusion | flops 1080033280 | bytes 8916992 | tf_op jit(solution)/shard_map/jvp()/dot_general | solution.py:44
  89.2 4.8 %select_convert_fusion = (bf16[4,512,512]{2,1,0:T(8,128)(2,1)S(1)}, f32[4,512,512]{2,1,0:T(8,128)}) fusion(pred[512,512]{1,0:T(8,128)(4,1)S(1)} %fusion.21, bf16[512,4,128]{0,2,1:T(8,128)(2,1)} %bitcast.68, bf16[512,4,128]{0,2,1:T(8,128)(2,1)} %bitcast.70), kind=kOutput, calls=%fused_computation.12 | convolution fusion | flops 275775488 | bytes 7602176 | tf_op jit(solution)/shard_map/jvp(qhd,khd->hqk)/dot_general | solution.py:53
  96.6 2.6 %copy.171 = f32[512,512]{1,0:T(8,128)} copy(f32[512,512]{0,1:T(8,128)} %bitcast.67) | data formatting | bytes 2097152 | tf_op jit(solution)/shard_map/jvp()/reshape | solution.py:60
  99.2 2.3 multiply_reduce_fusion
  102.2 3.0 %fusion.39 = (f32[512]{0:T(512)S(1)}, f32[512,512]{1,0:T(8,128)S(1)}, bf16[512,512]{1,0:T(8,128)(2,1)}, bf16[512,512]{1,0:T(8,128)(2,1)}) fusion(f32[512]{0:T(512)S(1)} %get-tuple-element.51, f32[512,512]{1,0:T(8,128)} %copy.171, f32[512]{0:T(512)S(1)} %broadcast_multiply_fusion, f32[512]{0:T(512)S(1)} %get-tuple-element.52, bf16[512,2048]{1,0:T(8,128)(2,1)} %copy-done.6, ...), kind=kLoop, calls=%fused_computation.95 | loop fusion | flops 3669504 | bytes 4202496 | tf_op jit(solution)/shard_map/transpose(jvp())/reduce_sum | solution.py:15
  108.2 4.4 %fusion.4 = bf16[4,512,512]{2,1,0:T(8,128)(2,1)S(1)} fusion(f32[4,512,512]{2,1,0:T(8,128)} %get-tuple-element.58, pred[512,512]{1,0:T(8,128)(4,1)S(1)} %fusion.21, bf16[4,128,512]{2,1,0:T(8,128)(2,1)} %bitcast.72, bf16[64,4,8,128]{3,2,1,0:T(8,128)(2,1)S(1)} %get-tuple-element.47), kind=kOutput, calls=%fused_computation.10 | convolution fusion | flops 283115520 | bytes 7602176 | tf_op jit(solution)/shard_map/transpose(jvp(hqk,khd->qhd))/dot_general | solution.py:58
  122.1 3.5 %fusion = bf16[512,2048]{1,0:T(8,128)(2,1)S(1)} fusion(f32[512,2048]{1,0:T(8,128)} %get-tuple-element.56, bf16[512,512]{1,0:T(8,128)(2,1)} %get-tuple-element.50, bf16[512,512]{1,0:T(8,128)(2,1)} %copy.175, bf16[512,512]{1,0:T(8,128)(2,1)} %copy.174, bf16[512,512]{1,0:T(8,128)(2,1)S(1)} %copy.173), kind=kLoop, calls=%fused_computation.6 | loop fusion | flops 18874368 | bytes 8388608 | tf_op jit(solution)/shard_map/transpose(jvp(jit(silu)))/add_any | solution.py:44
  134.7 6.9 %all-to-all-start.4 = ((bf16[64,4,2,512]{3,2,1,0:T(2,128)(2,1)}), bf16[64,4,2,512]{3,2,1,0:T(2,128)(2,1)S(1)}, u32[]{:S(2)}, u32[]{:S(2)}) async-start(bf16[64,4,2,512]{3,2,1,0:T(2,128)(2,1)} %reshape.212), calls=%async_computation.4 | async-start | bytes 1048576 | tf_op jit(solution)/shard_map/all_to_all | solution.py:95
  141.6 2.5 %fusion.9 = bf16[3072,512]{1,0:T(8,128)(2,1)} fusion(bf16[3072,512]{1,0:T(8,128)(2,1)} %slice_dynamic-update-slice_fusion, bf16[512,512]{1,0:T(8,128)(2,1)} %get-tuple-element.42, bf16[512,512]{1,0:T(8,128)(2,1)} %param.17), kind=kOutput, calls=%fused_computation.38 | convolution fusion | flops 268697600 | bytes 1572864 | tf_op jit(solution)/shard_map/transpose(jvp())/dot_general | solution.py:67
  146.9 64.8 %shard_map.128 = bf16[3072,512]{1,0:T(8,128)(2,1)} custom-call(bf16[3072,512]{1,0:T(8,128)(2,1)} %broadcast_dynamic-update-slice_fusion.g), custom_call_target="tpu_custom_call" | custom-call | tf_op jit(solution)/shard_map/pallas_call | solution.py:296
  211.8 2.9 %convert_element_type.129 = f32[3072,512]{1,0:T(8,128)S(1)} convert(bf16[3072,512]{1,0:T(8,128)(2,1)} %shard_map.128) | non-fusion elementwise | flops 1572864 | bytes 9437184 | tf_op jit(solution)/shard_map/convert_element_type | solution.py:339
  216.0 2.1 copy-done.2
  219.1 2.3 fusion.40
  222.6 3.7 %all-to-all-start.5 = ((bf16[64,4,2,512]{3,2,0,1:T(2,128)(2,1)}), bf16[64,4,2,512]{3,2,0,1:T(2,128)(2,1)S(1)}, u32[]{:S(2)}, u32[]{:S(2)}) async-start(bf16[64,4,2,512]{3,2,0,1:T(2,128)(2,1)} %copy.164), calls=%async_computation.5 | async-start | bytes 1048576 | tf_op jit(solution)/shard_map/all_to_all | solution.py:94
  230.3 4.7 %maximum_multiply_fusion = f32[512,2048]{1,0:T(8,128)} fusion(f32[512,512]{1,0:T(8,128)} %get-tuple-element.46, f32[512,512]{1,0:T(8,128)} %get-tuple-element.45, f32[512,512]{1,0:T(8,128)} %get-tuple-element.44, f32[512,512]{1,0:T(8,128)} %get-tuple-element.43), kind=kLoop, calls=%fused_computation.11 | loop fusion | flops 4194304 | bytes 8388608 | tf_op jit(solution)/shard_map/mul | solution.py:349
  237.6 2.9 %reshape.226 = f32[512,512]{1,0:T(8,128)} reshape(f32[64,4,2,512]{3,2,1,0:T(2,128)} %copy.166) | data formatting | bytes 2097152 | tf_op jit(solution)/shard_map/convert_element_type | solution.py:346
  240.6 4.9 %scatter_custom_fusion = f32[128,512]{1,0:T(8,128)} fusion(s32[512]{0:T(512)} %bitcast.79, f32[512,512]{1,0:T(8,128)} %reshape.226, f32[]{:T(128)} %constant.15.clone.1), kind=kCustom, calls=%fused_computation.78 | custom fusion | flops 262144 | bytes 262656 | tf_op jit(solution)/shard_map/scatter-add | solution.py:346
  (104 shorter events, 58.3 us)
Async XLA Ops:
  0.6 78.2 %copy-start = (bf16[512,2048]{1,0:T(8,128)(2,1)S(1)}, bf16[512,2048]{1,0:T(8,128)(2,1)}, u32[]{:S(2)}) copy-start(bf16[512,2048]{1,0:T(8,128)(2,1)} %param.15) | copy-start | bytes 6291460
  0.6 43.5 %copy-start.17 = (s32[1,4]{1,0:T(1,128)S(1)}, s32[1,4]{1,0:T(1,128)}, u32[]{:S(2)}) copy-start(s32[1,4]{1,0:T(1,128)} %param.12) | copy-start | bytes 52
  33.8 13.5 %copy-start.14 = (bf16[256,512]{1,0:T(8,128)(2,1)S(1)}, bf16[256,512]{1,0:T(8,128)(2,1)}, u32[]{:S(2)}) copy-start(bf16[256,512]{1,0:T(8,128)(2,1)} %param.14) | copy-start | bytes 786436
  38.0 38.5 %copy-start.15 = (s32[512]{0:T(512)S(1)}, s32[512]{0:T(512)}, u32[]{:S(2)}) copy-start(s32[512]{0:T(512)} %param.11) | copy-start | bytes 6148
  38.0 23.4 %all-to-all-start.2 = ((bf16[64,4,2,512]{3,2,1,0:T(2,128)(2,1)}), bf16[64,4,2,512]{3,2,1,0:T(2,128)(2,1)S(1)}, u32[]{:S(2)}, u32[]{:S(2)}) async-start(bf16[64,4,2,512]{3,2,1,0:T(2,128)(2,1)} %reshape.215), calls=%async_computation.2 | async-start | bytes 1048576 | tf_op jit(solution)/shard_map/all_to_all | solution.py:84
  62.5 12.6 %all-to-all-start.3 = ((bf16[64,4,2,512]{3,2,0,1:T(2,128)(2,1)}), bf16[64,4,2,512]{3,2,0,1:T(2,128)(2,1)S(1)}, u32[]{:S(2)}, u32[]{:S(2)}) async-start(bf16[64,4,2,512]{3,2,0,1:T(2,128)(2,1)} %copy.146), calls=%async_computation.3 | async-start | bytes 1048576 | tf_op jit(solution)/shard_map/all_to_all | solution.py:83
  82.6 1.3 copy-start.6
  94.0 2.6 %copy-start.4 = (bf16[4,512,512]{2,1,0:T(8,128)(2,1)}, bf16[4,512,512]{2,1,0:T(8,128)(2,1)S(1)}, u32[]{:S(2)}) copy-start(bf16[4,512,512]{2,1,0:T(8,128)(2,1)S(1)} %get-tuple-element.57) | copy-start | bytes 6291460
  94.9 1.0 copy-start.3
  108.2 4.5 %copy-start.9 = (bf16[512,512]{0,1:T(8,128)(2,1)S(1)}, bf16[512,512]{0,1:T(8,128)(2,1)}, u32[]{:S(2)}) copy-start(bf16[512,512]{0,1:T(8,128)(2,1)} %copy.176) | copy-start | bytes 1572868
  108.2 5.7 %copy-start.10 = (bf16[512,512]{0,1:T(8,128)(2,1)S(1)}, bf16[512,512]{0,1:T(8,128)(2,1)}, u32[]{:S(2)}) copy-start(bf16[512,512]{0,1:T(8,128)(2,1)} %copy.177) | copy-start | bytes 1572868
  112.6 2.9 %copy-start.5 = (bf16[4,512,512]{2,1,0:T(8,128)(2,1)S(1)}, bf16[4,512,512]{2,1,0:T(8,128)(2,1)}, u32[]{:S(2)}) copy-start(bf16[4,512,512]{2,1,0:T(8,128)(2,1)} %copy-done.4) | copy-start | bytes 6291460
  112.6 2.9 %copy-start.11 = (bf16[512,512]{0,1:T(8,128)(2,1)S(1)}, bf16[512,512]{0,1:T(8,128)(2,1)}, u32[]{:S(2)}) copy-start(bf16[512,512]{0,1:T(8,128)(2,1)} %copy.172) | copy-start | bytes 1572868
  128.2 3.7 %copy-start.8 = (bf16[512,512]{0,1:T(8,128)(2,1)S(1)}, bf16[512,512]{0,1:T(8,128)(2,1)}, u32[]{:S(2)}) copy-start(bf16[512,512]{0,1:T(8,128)(2,1)} %copy.163) | copy-start | bytes 1572868
  128.2 4.8 %copy-start.16 = (s32[512]{0:T(512)S(1)}, s32[512]{0:T(512)}, u32[]{:S(2)}) copy-start(s32[512]{0:T(512)} %param.11) | copy-start | bytes 6148
  132.2 0.8 copy-start.7
  134.7 86.8 %all-to-all-start.4 = ((bf16[64,4,2,512]{3,2,1,0:T(2,128)(2,1)}), bf16[64,4,2,512]{3,2,1,0:T(2,128)(2,1)S(1)}, u32[]{:S(2)}, u32[]{:S(2)}) async-start(bf16[64,4,2,512]{3,2,1,0:T(2,128)(2,1)} %reshape.212), calls=%async_computation.4 | async-start | bytes 1048576 | tf_op jit(solution)/shard_map/all_to_all | solution.py:95
  211.7 2.9 %copy-start.12 = (bf16[512,512]{1,0:T(8,128)(2,1)S(1)}, bf16[512,512]{1,0:T(8,128)(2,1)}, u32[]{:S(2)}) copy-start(bf16[512,512]{1,0:T(8,128)(2,1)} %param.16) | copy-start | bytes 1572868
  211.7 2.9 %copy-start.13 = (bf16[512,512]{1,0:T(8,128)(2,1)S(1)}, bf16[512,512]{1,0:T(8,128)(2,1)}, u32[]{:S(2)}) copy-start(bf16[512,512]{1,0:T(8,128)(2,1)} %get-tuple-element.42) | copy-start | bytes 1572868
  214.7 3.4 %copy-start.2 = (f32[3072,512]{1,0:T(8,128)}, f32[3072,512]{1,0:T(8,128)S(1)}, u32[]{:S(2)}) copy-start(f32[3072,512]{1,0:T(8,128)S(1)} %convert_element_type.129) | copy-start | bytes 18874372
  214.7 4.5 %copy-start.1 = (bf16[3072,512]{1,0:T(8,128)(2,1)S(1)}, bf16[3072,512]{1,0:T(8,128)(2,1)}, u32[]{:S(2)}) copy-start(bf16[3072,512]{1,0:T(8,128)(2,1)} %shard_map.128) | copy-start | bytes 9437188
  222.6 13.0 %all-to-all-start.5 = ((bf16[64,4,2,512]{3,2,0,1:T(2,128)(2,1)}), bf16[64,4,2,512]{3,2,0,1:T(2,128)(2,1)S(1)}, u32[]{:S(2)}, u32[]{:S(2)}) async-start(bf16[64,4,2,512]{3,2,0,1:T(2,128)(2,1)} %copy.164), calls=%async_computation.5 | async-start | bytes 1048576 | tf_op jit(solution)/shard_map/all_to_all | solution.py:94

commit v2 on v1

--- a/solution.py
+++ b/solution.py
@@ -68,39 +68,6 @@
     ).astype(jnp.bfloat16)
 
 
-def send_asked(wanted):
-    result = lax.all_to_all(
-        lax.all_to_all(wanted, "dp", split_axis=0, concat_axis=0, tiled=True),
-        "rep",
-        split_axis=1,
-        concat_axis=1,
-        tiled=True,
-    )
-    return result
-
-
-def send_fetched(fetched):
-    result = lax.all_to_all(
-        lax.all_to_all(fetched, "dp", split_axis=0, concat_axis=0, tiled=True),
-        "rep",
-        split_axis=1,
-        concat_axis=1,
-        tiled=True,
-    )
-    return result
-
-
-def send_returned(gradients):
-    result = lax.all_to_all(
-        lax.all_to_all(gradients, "dp", split_axis=0, concat_axis=0, tiled=True),
-        "rep",
-        split_axis=1,
-        concat_axis=1,
-        tiled=True,
-    )
-    return result
-
-
 MESH = pl.DeviceIdType.MESH
 ROWS_ALL = 3072
 HALF = 1536
@@ -124,6 +91,180 @@
 
 def span(start, size):
     return pl.ds(pl.multiple_of(start, size), size)
+
+
+BLOCK = 128
+
+
+def seat(t):
+    return (t // 4, lax.rem(t, 4))
+
+
+def greet_all(me, count):
+    barrier = pltpu.get_barrier_semaphore()
+
+    def body(j, carry):
+        to = seat(lax.rem(me + j, count))
+        pl.semaphore_signal(barrier, inc=1, device_id=to, device_id_type=MESH)
+        return carry
+
+    lax.fori_loop(1, count, body, 0)
+    pl.semaphore_wait(barrier, count - 1)
+
+
+def row_numbers(asked, first, sources):
+    count = asked.shape[0]
+    rows = sources * 8
+    lanes = asked.shape[-1]
+    table = asked.reshape(count, lanes).astype(jnp.float32).astype(jnp.bfloat16)
+    row = lax.broadcasted_iota(jnp.int32, (rows, count), 0) // 8 + first
+    source = lax.broadcasted_iota(jnp.int32, (rows, count), 1)
+    spread = jnp.where(row == source, 1.0, 0.0).astype(jnp.bfloat16)
+    both = jnp.dot(spread, table, preferred_element_type=jnp.float32)
+    slot = lax.rem(lax.broadcasted_iota(jnp.int32, (rows, lanes), 0), 8) // 4
+    lane = lax.broadcasted_iota(jnp.int32, (rows, lanes), 1)
+    one = jnp.where(slot == lane, both, 0.0).astype(jnp.bfloat16)
+    ones = jnp.ones((lanes, lanes), jnp.bfloat16)
+    return jnp.dot(one, ones, preferred_element_type=jnp.float32)
+
+
+def pickers(numbers):
+    rows, lanes = numbers.shape
+    lane = lax.broadcasted_iota(jnp.int32, (rows, lanes), 1).astype(jnp.float32)
+    quarter = lax.rem(lax.broadcasted_iota(jnp.int32, (rows, lanes), 0), 4)
+    hit = jnp.where(numbers == lane, 1.0, 0.0)
+    return [jnp.where(quarter == k, hit, 0.0).astype(jnp.bfloat16) for k in range(4)]
+
+
+def fetch_kernel(req, table, arrived, asked, fetched, ssem, rsem):
+    count = req.shape[0]
+    me = lax.axis_index("dp") * 4 + lax.axis_index("rep")
+    greet_all(me, count)
+
+    def copy(src, dst, index, to):
+        return pltpu.make_async_remote_copy(
+            src_ref=src,
+            dst_ref=dst,
+            send_sem=ssem.at[index],
+            recv_sem=rsem.at[index],
+            device_id=to,
+            device_id_type=MESH,
+        )
+
+    def ask(j, carry):
+        t = lax.rem(me + j, count)
+        copy(req.at[t], asked.at[me], 0, seat(t)).start()
+        return carry
+
+    lax.fori_loop(1, count, ask, 0)
+    asked[pl.ds(me, 1)] = req[pl.ds(me, 1)]
+    every = asked.at[pl.ds(0, count - 1)]
+    copy(every, every, 0, seat(me)).wait_recv()
+
+    group = 32
+
+    def serve(i, carry):
+        first = lax.rem(me // group + i, count // group) * group
+        hits = pickers(row_numbers(asked[...], first, group))
+        rows = None
+        for k in range(4):
+            part = jnp.dot(
+                hits[k], table[:, k * BLOCK : (k + 1) * BLOCK], preferred_element_type=jnp.float32
+            )
+            rows = part if rows is None else rows + part
+        fetched[pl.ds(first, group)] = rows.reshape(group, 8, BLOCK).astype(jnp.bfloat16)
+
+        def hand(j, inner):
+            t = first + lax.rem(me + j, group)
+
+            @pl.when(t != me)
+            def _():
+                copy(fetched.at[t], arrived.at[me], 1, seat(t)).start()
+
+            return inner
+
+        lax.fori_loop(0, group, hand, 0)
+        return carry
+
+    lax.fori_loop(0, count // group, serve, 0)
+    arrived[pl.ds(me, 1)] = fetched[pl.ds(me, 1)]
+    every = req.at[pl.ds(0, count - 1)]
+    copy(every, every, 0, seat(me)).wait_send()
+    every = arrived.at[pl.ds(0, count - 1)]
+    copy(every, every, 1, seat(me)).wait_recv()
+    every = fetched.at[pl.ds(0, count - 1)]
+    copy(every, every, 1, seat(me)).wait_send()
+
+
+def fetch_rows(req, table):
+    vmem = pl.BlockSpec(memory_space=pltpu.VMEM)
+    count = req.shape[0]
+    return pl.pallas_call(
+        fetch_kernel,
+        out_shape=(
+            jax.ShapeDtypeStruct((count, 8, BLOCK), jnp.bfloat16),
+            jax.ShapeDtypeStruct((count, 1, BLOCK), jnp.int32),
+        ),
+        in_specs=[vmem, vmem],
+        out_specs=(vmem, vmem),
+        scratch_shapes=[
+            pltpu.VMEM((count, 8, BLOCK), jnp.bfloat16),
+            pltpu.SemaphoreType.DMA((2,)),
+            pltpu.SemaphoreType.DMA((2,)),
+        ],
+        compiler_params=pltpu.CompilerParams(collective_id=1, has_side_effects=True),
+    )(req, table)
+
+
+def finish_kernel(sums, returned, asked, table_out, leaf_out, in_out, out_out):
+    count = asked.shape[0]
+    share = 1.0 / count
+    group = 64
+    table_out[...] = jnp.zeros_like(table_out)
+
+    def gather(i, carry):
+        first = i * group
+        hits = pickers(row_numbers(asked[...], first, group))
+        rows = returned[pl.ds(first, group)].reshape(group * 8, BLOCK)
+        for k in range(4):
+            table_out[:, k * BLOCK : (k + 1) * BLOCK] += lax.dot_general(
+                hits[k], rows, (((0,), (0,)), ((), ())), preferred_element_type=jnp.float32
+            )
+        return carry
+
+    lax.fori_loop(0, count // group, gather, 0)
+    width = 512
+
+    def scale(first, dst, rows, column):
+        def body(i, carry):
+            at = pl.multiple_of(i * 64, 64)
+            dst[pl.ds(at, 64), column : column + width] = (
+                sums[pl.ds(pl.multiple_of(first + i * 64, 64), 64), :].astype(jnp.float32) * share
+            )
+            return carry
+
+        lax.fori_loop(0, rows // 64, body, 0)
+
+    for i in range(4):
+        scale(i * width, in_out, width, i * width)
+    scale(2048, out_out, 512, 0)
+    scale(2560, leaf_out, 256, 0)
+
+
+def finish(sums, returned, asked):
+    vmem = pl.BlockSpec(memory_space=pltpu.VMEM)
+    f32 = jnp.float32
+    return pl.pallas_call(
+        finish_kernel,
+        out_shape=(
+            jax.ShapeDtypeStruct((128, 512), f32),
+            jax.ShapeDtypeStruct((256, 512), f32),
+            jax.ShapeDtypeStruct((512, 2048), f32),
+            jax.ShapeDtypeStruct((512, 512), f32),
+        ),
+        in_specs=[vmem] * 3,
+        out_specs=(vmem,) * 4,
+    )(sums, returned, asked)
 
 
 def add_into(dst, start, sources, rows, step):
@@ -138,7 +279,7 @@
     lax.fori_loop(0, rows // step, body, 0)
 
 
-def sum_kernel(g, out, w, r0, r1a, r1b, r2a, r2b, rz, ssem, rsem):
+def sum_kernel(g, back, out, returned, w, r0, r1a, r1b, r2a, r2b, rz, ssem, rsem, bsem):
     x, y, z, c = here()
     p1 = (1 - c) * x + c * y
     p2 = c * x + (1 - c) * y
@@ -153,11 +294,9 @@
         return device(x, y, lax.rem(z + d, 8), c)
 
     partner = device(x, y, z, 1 - c)
-    barrier = pltpu.get_barrier_semaphore()
-    peers = [partner, axis1(1), axis1(3), axis2(1), axis2(3)] + [axisz(j) for j in range(1, 8)]
-    for peer in peers:
-        pl.semaphore_signal(barrier, inc=1, device_id=peer, device_id_type=MESH)
-    pl.semaphore_wait(barrier, len(peers))
+    count = back.shape[0]
+    me = lax.axis_index("dp") * 4 + x
+    greet_all(me, count)
 
     started = []
 
@@ -189,6 +328,24 @@
     for k, off in enumerate(order):
         q = lax.rem(p2 + off, 4)
         send(g.at[span(other + q * R1, R1), :], r0.at[span(q * R1, R1), :], k, partner)
+
+    def back_copy(src, dst, to):
+        return pltpu.make_async_remote_copy(
+            src_ref=src,
+            dst_ref=dst,
+            send_sem=bsem.at[0],
+            recv_sem=bsem.at[1],
+            device_id=to,
+            device_id_type=MESH,
+        )
+
+    def give_back(j, carry):
+        t = lax.rem(me + j, count)
+        back_copy(back.at[t], returned.at[me], seat(t)).start()
+        return carry
+
+    lax.fori_loop(1, count, give_back, 0)
+    returned[pl.ds(me, 1)] = back[pl.ds(me, 1)]
 
     def ring_sum(pos, first, rows, right, left, ra, rb, index, local, own):
         half = rows // 2
@@ -288,16 +445,23 @@
         arrive(out.at[span(other + q * R1, R1), :], 34 + k)
     for copy in started:
         copy.wait_send()
-
-
-def sum_all(g):
+    every = returned.at[pl.ds(0, count - 1)]
+    back_copy(every, every, seat(me)).wait_recv()
+    every = back.at[pl.ds(0, count - 1)]
+    back_copy(every, every, seat(me)).wait_send()
+
+
+def sum_all(g, back):
     vmem = pl.BlockSpec(memory_space=pltpu.VMEM)
     bf16 = jnp.bfloat16
     return pl.pallas_call(
         sum_kernel,
-        out_shape=jax.ShapeDtypeStruct((ROWS_ALL, 512), bf16),
-        in_specs=[vmem],
-        out_specs=vmem,
+        out_shape=(
+            jax.ShapeDtypeStruct((ROWS_ALL, 512), bf16),
+            jax.ShapeDtypeStruct(back.shape, bf16),
+        ),
+        in_specs=[vmem, vmem],
+        out_specs=(vmem, vmem),
         scratch_shapes=[
             pltpu.VMEM((HALF, 512), bf16),
             pltpu.VMEM((HALF, 512), bf16),
@@ -308,21 +472,20 @@
             pltpu.VMEM((7, RZ, 128), bf16),
             pltpu.SemaphoreType.DMA((38,)),
             pltpu.SemaphoreType.DMA((38,)),
+            pltpu.SemaphoreType.DMA((2,)),
         ],
         compiler_params=pltpu.CompilerParams(collective_id=0, has_side_effects=True),
-    )(g)
+    )(g, back)
 
 
 def on_device(
     item_table, requests, event_slot, lengths, leaf_ids, leaf_table, w_in, w_out, cotangent
 ):
-    data_count = lax.axis_size("dp")
-    replica_count = lax.axis_size("rep")
     width = item_table.shape[1]
-    wanted = requests.reshape(data_count, replica_count, -1)
-    asked = send_asked(wanted)
-    fetched = item_table[asked]
-    arrived = send_fetched(fetched).reshape(-1, width)
+    count = requests.shape[1]
+    asks = jnp.pad(requests.reshape(count, 1, 2), ((0, 0), (0, 0), (0, BLOCK - 2)))
+    blocks, asked = fetch_rows(asks, item_table)
+    arrived = blocks.reshape(-1, width)
 
     def local_front(rows, table_leaf, weight_in):
         return front(rows, event_slot, lengths[0], leaf_ids, table_leaf, weight_in)
@@ -331,22 +494,12 @@
     output, pull_back = jax.vjp(back, inputs, gated, w_out)
     d_inputs, d_gated, d_out = pull_back(cotangent)
     d_rows, d_leaf, d_in = pull_front((d_inputs, d_gated))
-    returned = send_returned(d_rows.reshape(data_count, replica_count, -1, width))
     stacked = jnp.concatenate(
         [d_in[:, i * width : (i + 1) * width] for i in range(4)]
         + [d_out, d_leaf, jnp.zeros((ROWS_ALL - 2816, width), jnp.bfloat16)]
     )
-    sums = sum_all(stacked).astype(jnp.float32)
-    in_sum = jnp.concatenate([sums[i * width : (i + 1) * width] for i in range(4)], axis=1)
-    out_sum = sums[2048:2560]
-    leaf_sum = sums[2560:2816]
-    table_grad = (
-        jnp.zeros(item_table.shape, jnp.float32)
-        .at[asked.reshape(-1)]
-        .add(returned.reshape(-1, width).astype(jnp.float32))
-    )
-    share = 1.0 / (data_count * replica_count)
-    return (output, table_grad, leaf_sum * share, in_sum * share, out_sum * share)
+    sums, returned = sum_all(stacked, d_rows.reshape(blocks.shape))
+    return (output, *finish(sums, returned, asked))
 
 
 def solution(mesh):

time: 247 us -> 203 us (0.82)
  Pallas kernels: 64.8 us -> 125 us
  blocking collectives: 30.7 us -> 0 us
  waiting for transfers between devices: 21.4 us -> 0 us
  starting transfers between devices: 20.3 us -> 0 us
  local copies, waits for them, and re-layouts: 46.8 us -> 30.1 us
  other arithmetic: 27.8 us -> 11.2 us
    pallas_call x1 -> x3, Pallas kernels: 64.8 us -> 125 us  [the longest x1 71.1 us: sum_all(): pl.pallas_call(sum_kernel, out_shape=(jax.ShapeDtypeStruct((ROWS_ALL, 512...]
    all_to_all x2 -> x0, blocking collectives: 30.7 us -> none  [the longest x1 22.7 us: send_asked(): lax.all_to_all(wanted, 'dp', split_axis=0, concat_axis=0, tiled=True)]
    all_to_all x4 -> x0, waiting for transfers between devices: 21.4 us -> none  [the longest x1 12.8 us: send_fetched(): lax.all_to_all(fetched, 'dp', split_axis=0, concat_axis=0, tiled=True)]
    all_to_all x4 -> x0, starting transfers between devices: 20.3 us -> none  [the longest x1 6.94 us: send_returned(): lax.all_to_all(gradients, 'dp', split_axis=0, concat_axis=0, tiled=True)]
    mul x3 -> x0, other arithmetic: 7.65 us -> none  [the longest x1 4.71 us: on_device(): in_sum * share]
    scatter-add x1 -> x0, other arithmetic: 4.91 us -> none  [on_device(): table_grad = jnp.zeros(item_table.shape, jnp.float32).at[asked.reshape(-1...]
    convert_element_type x2 -> x0, local copies, waits for them, and re-layouts: 4.77 us -> none  [on_device(): returned.reshape(-1, width).astype(jnp.float32)]
    gather x2 -> x0, local copies, waits for them, and re-layouts: 3.9 us -> none  [on_device(): fetched = item_table[asked]]
  transfers between devices with their start and end apart: 4 -> 0, of which waited for: 3 -> 0; matrix products, arithmetic and copies ran while one was open for 11% -> 0% of each run, Pallas kernels for 26% -> 0%
where the time goes in v2:
time: 203 us; the launch traced here: 202 us
  Pallas kernels  125 us (62%)
  matrix products  34.7 us (17%)
  local copies, waits for them, and re-layouts  30.1 us (15%)
  other arithmetic  11.2 us (6%)
    pallas_call x1, Pallas kernels, sum_all(): pl.pallas_call(sum_kernel, out_shape=(jax.ShapeDtypeStruct((ROWS_ALL, 512...  71.1 us
    pallas_call x1, Pallas kernels, fetch_rows(): pl.pallas_call(fetch_kernel, out_shape=(jax.ShapeDtypeStruct((count, 8, B...  45 us
    unnamed x38, local copies, waits for them, and re-layouts  11.9 us
    dot_general x3, matrix products, front(): jnp.einsum('qhd,khd->hqk', query_heads, key_heads, preferred_element_type...  9.3 us
    pallas_call x1, Pallas kernels, finish(): pl.pallas_call(finish_kernel, out_shape=(jax.ShapeDtypeStruct((128, 512),...  8.74 us
    dot_general x3, matrix products, front(): jnp.einsum('hqk,khd->qhd', weights, value_heads, preferred_element_type=j...  8.44 us
    dot_general x3, matrix products, front(): jnp.dot(normed, w_in, preferred_element_type=jnp.float32)  8 us
    dot_general x3, matrix products, back(): jnp.dot(gated, w_out, preferred_element_type=jnp.float32)  5.32 us

profile of v2, /device:TPU:1, one launch (start us, length us, event | category | flops | bytes accessed | tf_op | source)
XLA Modules:
  0.0 201.8 jit_solution(16391694075219862193)
XLA Ops:
  2.4 45.0 %shard_map.128 = (bf16[256,8,128]{2,1,0:T(8,128)(2,1)}, s32[256,1,128]{2,1,0:T(1,128)}) custom-call(s32[256,1,128]{2,1,0:T(1,128)} %pad.16.req, bf16[128,512]{1,0:T(8,128)(2,1)} %table.1), custom_call_target="tpu_custom_call" | custom-call | tf_op jit(solution)/shard_map/pallas_call | solution.py:202
  47.4 1.4 reshape.166
  49.7 1.3 fusion.39
  51.9 3.9 %multiply_convert_fusion = (bf16[512,2048]{1,0:T(8,128)(2,1)S(1)}, f32[512,2048]{1,0:T(8,128)}) fusion(bf16[512,2048]{1,0:T(8,128)(2,1)S(1)} %copy-done, bf16[512,512]{0,1:T(8,128)(2,1)S(1)} %get-tuple-element.46, f32[512]{0:T(512)S(1)} %fusion.35, f32[512]{0:T(512)S(1)} %broadcast_multiply_fusion.1), kind=kOutput, calls=%fused_computation.11 | convolution fusion | flops 1080033280 | bytes 8916992 | tf_op jit(solution)/shard_map/jvp()/dot_general | solution.py:44
  55.7 1.3 copy-done.5
  58.2 2.0 %copy.74 = bf16[512,512]{0,1:T(8,128)(2,1)} copy(bf16[512,512]{1,0:T(8,128)(2,1)} %get-tuple-element.41) | data formatting | bytes 1048576 | tf_op jit(solution)/shard_map/jvp()/reshape | solution.py:51
  60.3 2.0 %copy.75 = bf16[512,512]{0,1:T(8,128)(2,1)} copy(bf16[512,512]{1,0:T(8,128)(2,1)} %get-tuple-element.40) | data formatting | bytes 1048576 | tf_op jit(solution)/shard_map/jvp()/reshape | solution.py:52
  62.8 4.8 %select_convert_fusion = (bf16[4,512,512]{2,1,0:T(8,128)(2,1)S(1)}, f32[4,512,512]{2,1,0:T(8,128)}) fusion(pred[512,512]{1,0:T(8,128)(4,1)S(1)} %fusion.21, bf16[512,4,128]{0,2,1:T(8,128)(2,1)} %bitcast.65, bf16[512,4,128]{0,2,1:T(8,128)(2,1)} %bitcast.63), kind=kOutput, calls=%fused_computation.9 | convolution fusion | flops 275775488 | bytes 7602176 | tf_op jit(solution)/shard_map/jvp(qhd,khd->hqk)/dot_general | solution.py:53
  70.2 2.6 %copy.69 = f32[512,512]{1,0:T(8,128)} copy(f32[512,512]{0,1:T(8,128)} %bitcast.62) | data formatting | bytes 2097152 | tf_op jit(solution)/shard_map/jvp()/reshape | solution.py:60
  72.8 2.4 %multiply_reduce_fusion = (f32[512]{0:T(512)S(1)}, bf16[512,512]{1,0:T(8,128)(2,1)S(1)}) fusion(f32[512,512]{1,0:T(8,128)} %copy.69, f32[512]{0:T(512)S(1)} %broadcast_multiply_fusion, bf16[512,2048]{1,0:T(8,128)(2,1)} %copy-done.5, bf16[512,512]{1,0:T(8,128)(2,1)} %param.17, bf16[512,512]{1,0:T(8,128)(2,1)} %param.16), kind=kOutput, calls=%fused_computation.49 | convolution fusion | flops 270269952 | bytes 3149824 | tf_op jit(solution)/shard_map/transpose(jvp())/dot_general | solution.py:67
  75.2 2.6 %fusion.37 = (f32[512]{0:T(512)S(1)}, f32[512,512]{1,0:T(8,128)S(1)}, bf16[512,512]{1,0:T(8,128)(2,1)}, bf16[512,512]{1,0:T(8,128)(2,1)}) fusion(f32[512]{0:T(512)S(1)} %get-tuple-element.43, f32[512,512]{1,0:T(8,128)S(1)} %copy-done.2, f32[512]{0:T(512)S(1)} %broadcast_multiply_fusion, f32[512]{0:T(512)S(1)} %get-tuple-element.44, ...), kind=kLoop, calls=%fused_computation.84 | loop fusion | flops 3669504 | bytes 4202496 | tf_op jit(solution)/shard_map/transpose(jvp())/reduce_sum | solution.py:15
  78.8 2.1 %copy.70 = bf16[512,512]{0,1:T(8,128)(2,1)} copy(bf16[512,512]{1,0:T(8,128)(2,1)} %broadcast_add_fusion) | data formatting | bytes 1048576 | tf_op jit(solution)/shard_map/transpose(jvp())/reshape | solution.py:60
  80.9 4.6 %fusion.4 = bf16[4,512,512]{2,1,0:T(8,128)(2,1)S(1)} fusion(f32[4,512,512]{2,1,0:T(8,128)} %get-tuple-element.50, pred[512,512]{1,0:T(8,128)(4,1)S(1)} %fusion.21, bf16[4,128,512]{2,1,0:T(8,128)(2,1)} %bitcast.67, bf16[64,4,8,128]{3,2,1,0:T(8,128)(2,1)S(1)} %get-tuple-element.39), kind=kOutput, calls=%fused_computation.8 | convolution fusion | flops 283115520 | bytes 7602176 | tf_op jit(solution)/shard_map/transpose(jvp(hqk,khd->qhd))/dot_general | solution.py:58
  85.5 1.3 copy-done.3
  89.4 3.3 %fusion.41 = bf16[4,512,128]{1,2,0:T(8,128)(2,1)} fusion(bf16[4,512,512]{2,1,0:T(8,128)(2,1)} %copy-done.3, bf16[512,4,128]{0,2,1:T(8,128)(2,1)} %bitcast.64), kind=kOutput, calls=%fused_computation.88 | convolution fusion | flops 268435456 | bytes 3145728 | tf_op jit(solution)/shard_map/transpose(jvp(qhd,khd->hqk))/dot_general | solution.py:53
  92.6 2.1 %copy.72 = bf16[512,512]{1,0:T(8,128)(2,1)} copy(bf16[512,512]{0,1:T(8,128)(2,1)} %bitcast.69) | data formatting | bytes 1048576 | tf_op jit(solution)/shard_map/transpose(jvp())/reshape | solution.py:51
  94.7 3.0 %fusion.40 = bf16[4,128,512]{2,1,0:T(8,128)(2,1)} fusion(bf16[4,128,512]{2,1,0:T(8,128)(2,1)} %bitcast.68, bf16[4,512,512]{2,1,0:T(8,128)(2,1)} %copy-done.4), kind=kOutput, calls=%fused_computation.87 | convolution fusion | flops 268435456 | bytes 3145728 | tf_op jit(solution)/shard_map/transpose(jvp(hqk,khd->qhd))/dot_general | solution.py:58
  97.7 2.0 %copy.73 = bf16[512,512]{1,0:T(8,128)(2,1)} copy(bf16[512,512]{0,1:T(8,128)(2,1)} %bitcast.70) | data formatting | bytes 1048576 | tf_op jit(solution)/shard_map/transpose(jvp())/reshape | solution.py:50
  99.8 3.5 %fusion = bf16[512,2048]{1,0:T(8,128)(2,1)S(1)} fusion(f32[512,2048]{1,0:T(8,128)} %get-tuple-element.48, bf16[512,512]{1,0:T(8,128)(2,1)} %get-tuple-element.42, bf16[512,512]{1,0:T(8,128)(2,1)} %copy.73, bf16[512,512]{1,0:T(8,128)(2,1)} %copy.72, bf16[512,512]{1,0:T(8,128)(2,1)S(1)} %copy.71), kind=kLoop, calls=%fused_computation.4 | loop fusion | flops 18874368 | bytes 8388608 | tf_op jit(solution)/shard_map/transpose(jvp(jit(silu)))/add_any | solution.py:44
  106.7 1.6 fusion.24
  108.2 2.9 %convolution_convert_fusion = bf16[512,2048]{1,0:T(8,128)(2,1)S(1)} fusion(bf16[512,2048]{1,0:T(8,128)(2,1)} %copy-done.9, bf16[512,512]{0,1:T(8,128)(2,1)S(1)} %get-tuple-element.46, f32[512]{0:T(512)S(1)} %fusion.35, f32[512]{0:T(512)S(1)} %broadcast_multiply_fusion.1), kind=kOutput, calls=%fused_computation.13 | convolution fusion | flops 1074790400 | bytes 4722688 | tf_op jit(solution)/shard_map/transpose(jvp())/dot_general | solution.py:44
  119.3 71.1 %shard_map.129 = (bf16[3072,512]{1,0:T(8,128)(2,1)}, bf16[256,8,128]{2,1,0:T(8,128)(2,1)}) custom-call(bf16[3072,512]{1,0:T(8,128)(2,1)} %broadcast_dynamic-update-slice_fusion.g, bf16[256,8,128]{2,1,0:T(8,128)(2,1)} %reshape.177.back), custom_call_target="tpu_custom_call" | custom-call | tf_op jit(solution)/shard_map/pallas_call | solution.py:457
  190.4 8.7 %shard_map.130 = (f32[128,512]{1,0:T(8,128)}, f32[256,512]{1,0:T(8,128)}, f32[512,2048]{1,0:T(8,128)}, f32[512,512]{1,0:T(8,128)}) custom-call(bf16[3072,512]{1,0:T(8,128)(2,1)} %get-tuple-element.14.sums, bf16[256,8,128]{2,1,0:T(8,128)(2,1)} %get-tuple-element.15.returned, s32[256,1,128]{2,1,0:T(1,128)} %get-tuple-element.16.asked), custom_call_target="tpu_custom_call" | custom-call | tf_op jit(solution)/shard_map/pallas_call | solution.py:257
  199.2 1.7 fusion.10
  (64 shorter events, 23.7 us)
Async XLA Ops:
  0.6 51.2 %copy-start = (bf16[512,2048]{1,0:T(8,128)(2,1)S(1)}, bf16[512,2048]{1,0:T(8,128)(2,1)}, u32[]{:S(2)}) copy-start(bf16[512,2048]{1,0:T(8,128)(2,1)} %param.15) | copy-start | bytes 6291460
  0.6 50.4 %copy-start.12 = (s32[512]{0:T(512)S(1)}, s32[512]{0:T(512)}, u32[]{:S(2)}) copy-start(s32[512]{0:T(512)} %param.11) | copy-start | bytes 6148
  55.7 1.3 copy-start.5
  55.7 6.6 %copy-start.14 = (s32[1,4]{1,0:T(1,128)S(1)}, s32[1,4]{1,0:T(1,128)}, u32[]{:S(2)}) copy-start(s32[1,4]{1,0:T(1,128)} %param.12) | copy-start | bytes 52
  67.6 2.6 %copy-start.4 = (bf16[4,512,512]{2,1,0:T(8,128)(2,1)}, bf16[4,512,512]{2,1,0:T(8,128)(2,1)S(1)}, u32[]{:S(2)}) copy-start(bf16[4,512,512]{2,1,0:T(8,128)(2,1)S(1)} %get-tuple-element.49) | copy-start | bytes 6291460
  68.4 1.0 copy-start.1
  72.8 2.4 %copy-start.11 = (f32[512]{0:T(512)S(1)}, f32[512]{0:T(512)}, u32[]{:S(2)}) copy-start(f32[512]{0:T(512)} %fusion.19) | copy-start | bytes 6148
  72.8 2.4 %copy-start.2 = (f32[512,512]{1,0:T(8,128)S(1)}, f32[512,512]{1,0:T(8,128)}, u32[]{:S(2)}) copy-start(f32[512,512]{1,0:T(8,128)} %copy.69) | copy-start | bytes 3145732
  80.9 6.0 %copy-start.7 = (bf16[512,512]{0,1:T(8,128)(2,1)S(1)}, bf16[512,512]{0,1:T(8,128)(2,1)}, u32[]{:S(2)}) copy-start(bf16[512,512]{0,1:T(8,128)(2,1)} %copy.74) | copy-start | bytes 1572868
  85.5 1.4 copy-start.3
  103.2 1.3 copy-start.9
  103.2 2.4 %copy-start.6 = (bf16[512,512]{1,0:T(8,128)(2,1)S(1)}, bf16[512,512]{1,0:T(8,128)(2,1)}, u32[]{:S(2)}) copy-start(bf16[512,512]{1,0:T(8,128)(2,1)} %param.17) | copy-start | bytes 1572868
  104.6 0.8 copy-start.8
  111.1 3.4 %copy-start.10 = (bf16[512,512]{1,0:T(8,128)(2,1)S(1)}, bf16[512,512]{1,0:T(8,128)(2,1)}, u32[]{:S(2)}) copy-start(bf16[512,512]{1,0:T(8,128)(2,1)} %get-tuple-element.38) | copy-start | bytes 1572868
  111.9 5.5 %copy-start.13 = (s32[512]{0:T(512)S(1)}, s32[512]{0:T(512)}, u32[]{:S(2)}) copy-start(s32[512]{0:T(512)} %param.11) | copy-start | bytes 6148

commit v3 on v2

--- a/solution.py
+++ b/solution.py
@@ -9,63 +9,6 @@
 
 
 epsilon = 1e-06
-
-
-def normalize(values):
-    center = values - jnp.mean(values, axis=-1, keepdims=True)
-    spread = jnp.mean(center * center, axis=-1, keepdims=True)
-    return center * lax.rsqrt(spread + epsilon)
-
-
-def visible(lengths, count):
-    ends = jnp.cumsum(lengths)
-    places = jnp.arange(count, dtype=jnp.int32)
-    segment = jnp.sum((places[:, None] >= ends[None, :]).astype(jnp.int32), axis=1)
-    same = segment[:, None] == segment[None, :]
-    return jnp.logical_and(same, places[None, :] <= places[:, None])
-
-
-def front(rows, event_slot, lengths, leaf_ids, leaf_table, w_in):
-    count = event_slot.shape[0]
-    picker = (event_slot[:, None] == jnp.arange(rows.shape[0], dtype=jnp.int32)[None, :]).astype(
-        jnp.bfloat16
-    )
-    leaves = leaf_table.shape[0] // leaf_ids.shape[1]
-    onehot = (
-        (leaf_ids[:, :, None] == jnp.arange(leaves, dtype=jnp.int32)[None, None, :])
-        .reshape(count, -1)
-        .astype(jnp.bfloat16)
-    )
-    inputs = (
-        jnp.dot(picker, rows, preferred_element_type=jnp.float32)
-        + jnp.dot(onehot, leaf_table, preferred_element_type=jnp.float32)
-    ).astype(jnp.bfloat16)
-    normed = normalize(inputs.astype(jnp.float32)).astype(jnp.bfloat16)
-    hidden = jax.nn.silu(jnp.dot(normed, w_in, preferred_element_type=jnp.float32)).astype(
-        jnp.bfloat16
-    )
-    width = w_in.shape[0]
-    head_size = width // HEADS
-    gates = hidden[:, 0:width]
-    value_heads = hidden[:, width : 2 * width].reshape(count, HEADS, head_size)
-    query_heads = hidden[:, 2 * width : 3 * width].reshape(count, HEADS, head_size)
-    key_heads = hidden[:, 3 * width : 4 * width].reshape(count, HEADS, head_size)
-    scores = jnp.einsum(
-        "qhd,khd->hqk", query_heads, key_heads, preferred_element_type=jnp.float32
-    ) * head_size ** (-0.5)
-    allowed = visible(lengths, count)
-    weights = jnp.where(allowed[None], jax.nn.silu(scores), 0.0).astype(jnp.bfloat16)
-    mixed = jnp.einsum(
-        "hqk,khd->qhd", weights, value_heads, preferred_element_type=jnp.float32
-    ).reshape(count, width)
-    gated = (normalize(mixed) * gates.astype(jnp.float32)).astype(jnp.bfloat16)
-    return (inputs, gated)
-
-
-def back(inputs, gated, w_out):
-    return (
-        jnp.dot(gated, w_out, preferred_element_type=jnp.float32) + inputs.astype(jnp.float32)
-    ).astype(jnp.bfloat16)
 
 
 MESH = pl.DeviceIdType.MESH
@@ -478,27 +421,256 @@
     )(g, back)
 
 
+TILE = 128
+
+
+def tn(a, b):
+    return lax.dot_general(a, b, (((0,), (0,)), ((), ())), preferred_element_type=jnp.float32)
+
+
+def nt(a, b):
+    return lax.dot_general(a, b, (((1,), (1,)), ((), ())), preferred_element_type=jnp.float32)
+
+
+def nn(a, b):
+    return jnp.dot(a, b, preferred_element_type=jnp.float32)
+
+
+def silu_and_slope(v):
+    half = 0.5 * v
+    t = jnp.tanh(half)
+    up = 1.0 + t
+    return half * up, 0.5 * up * (1.0 + half * (1.0 - t))
+
+
+def centered(values):
+    center = values - jnp.mean(values, axis=-1, keepdims=True)
+    spread = jnp.mean(center * center, axis=-1, keepdims=True)
+    scale = lax.rsqrt(spread + epsilon)
+    return center * scale, scale
+
+
+def norm_back(d, normal, scale):
+    mean = jnp.mean(d, axis=-1, keepdims=True)
+    along = jnp.mean(d * normal, axis=-1, keepdims=True)
+    return scale * (d - mean - normal * along)
+
+
+def layer_kernel(
+    lengths, slots, leaves, arrived, leaf_table, w_in, w_out, cotangent,
+    output, grads, back,
+    pick, onehot, flat, rows, inputs, normed, scale, hidden, slope, weights, bend, mixed, gated,
+    d_mixed, d_hidden, turned, d_inputs,
+):
+    f32, bf16 = jnp.float32, jnp.bfloat16
+    count, width = output.shape
+    steps = count // TILE
+    head = width // HEADS
+
+    def tile(r):
+        return pl.ds(pl.multiple_of(r * TILE, TILE), TILE)
+
+    def block(i):
+        return pl.ds(pl.multiple_of(i * width, width), width)
+
+    flat[...] = arrived[...].reshape(4 * count, 128).astype(f32)
+    for k in range(4):
+        rows[:, k * 128 : (k + 1) * 128] = flat[pl.ds(k, count, stride=4), :].astype(bf16)
+
+    def build(r, carry):
+        number = lax.broadcasted_iota(jnp.int32, (TILE, count), 0) + r * TILE
+        pick[tile(r), :] = jnp.where(number == slots[...], 1.0, 0.0).astype(bf16)
+        return carry
+
+    lax.fori_loop(0, steps, build, 0)
+    each = onehot.shape[0] // leaves.shape[0]
+    for t in range(leaves.shape[0]):
+        number = lax.broadcasted_iota(jnp.int32, (each, count), 0)
+        hit = jnp.where(number == leaves[t : t + 1, :], 1.0, 0.0)
+        onehot[t * each : (t + 1) * each, :] = hit.astype(bf16)
+
+    def front_step(r, carry):
+        at = tile(r)
+        x = (tn(pick[:, at], rows[...]) + tn(onehot[:, at], leaf_table[...])).astype(bf16)
+        inputs[at, :] = x
+        normal, factor = centered(x.astype(f32))
+        normal = normal.astype(bf16)
+        normed[at, :] = normal
+        scale[at, :] = factor
+        for i in range(4):
+            cut = slice(i * width, (i + 1) * width)
+            value, bent = silu_and_slope(nn(normal, w_in[:, cut]))
+            hidden[at, cut] = value.astype(bf16)
+            slope[at, cut] = bent
+        return carry
+
+    lax.fori_loop(0, steps, front_step, 0)
+
+    e1 = lengths[0, 0]
+    e2 = e1 + lengths[0, 1]
+    e3 = e2 + lengths[0, 2]
+    spans = [(max(0, i - 2), i + 1) for i in range(steps)]
+    seen = []
+    for i, (low, high) in enumerate(spans):
+        shape = (TILE, (high - low) * TILE)
+        row = lax.broadcasted_iota(jnp.int32, shape, 0) + i * TILE
+        column = lax.broadcasted_iota(jnp.int32, shape, 1) + low * TILE
+        first = jnp.where(row >= e1, e1, 0)
+        first = jnp.where(row >= e2, e2, first)
+        first = jnp.where(row >= e3, e3, first)
+        seen.append(jnp.logical_and(column >= first, column <= row))
+    factor = head ** (-0.5)
+
+    def lanes(part, h):
+        return pl.ds(pl.multiple_of(part * width + h * head, head), head)
+
+    def attend(h, carry):
+        for i, (low, high) in enumerate(spans):
+            at = slice(i * TILE, (i + 1) * TILE)
+            keys = slice(low * TILE, high * TILE)
+            wide = slice(0, (high - low) * TILE)
+            scores = nt(hidden[at, lanes(2, h)], hidden[keys, lanes(3, h)]) * factor
+            value, bent = silu_and_slope(scores)
+            value = jnp.where(seen[i], value, 0.0).astype(bf16)
+            weights[h, at, wide] = value
+            bend[h, at, wide] = jnp.where(seen[i], bent * factor, 0.0)
+            mixed[at, lanes(0, h)] = nn(value, hidden[keys, lanes(1, h)])
+        return carry
+
+    lax.fori_loop(0, HEADS, attend, 0)
+
+    def middle(r, carry):
+        at = tile(r)
+        normal, factor = centered(mixed[at, :])
+        gates = hidden[at, 0:width].astype(f32)
+        gate = (normal * gates).astype(bf16)
+        gated[at, :] = gate
+        output[at, :] = (nn(gate, w_out[...]) + inputs[at, :].astype(f32)).astype(bf16)
+        d_gated = nt(cotangent[at, :], w_out[...]).astype(bf16).astype(f32)
+        d_gates = (d_gated * normal).astype(bf16).astype(f32)
+        d_hidden[at, 0:width] = (d_gates * slope[at, 0:width]).astype(bf16)
+        d_mixed[at, :] = norm_back(d_gated * gates, normal, factor).astype(bf16)
+        return carry
+
+    lax.fori_loop(0, steps, middle, 0)
+
+    def attend_back(h, carry):
+        d_keys = [None] * steps
+        d_values = [None] * steps
+        for i, (low, high) in enumerate(spans):
+            at = slice(i * TILE, (i + 1) * TILE)
+            keys = slice(low * TILE, high * TILE)
+            wide = slice(0, (high - low) * TILE)
+            d_mix = d_mixed[at, lanes(0, h)]
+            d_weights = nt(d_mix, hidden[keys, lanes(1, h)]).astype(bf16).astype(f32)
+            d_scores = (d_weights * bend[h, at, wide]).astype(bf16)
+            d_queries = nn(d_scores, hidden[keys, lanes(3, h)]).astype(bf16).astype(f32)
+            d_hidden[at, lanes(2, h)] = (d_queries * slope[at, lanes(2, h)]).astype(bf16)
+            dk = tn(d_scores, hidden[at, lanes(2, h)])
+            dv = tn(weights[h, at, wide], d_mix)
+            for j in range(low, high):
+                cut = slice((j - low) * TILE, (j - low + 1) * TILE)
+                d_keys[j] = dk[cut] if d_keys[j] is None else d_keys[j] + dk[cut]
+                d_values[j] = dv[cut] if d_values[j] is None else d_values[j] + dv[cut]
+        for j in range(steps):
+            at = slice(j * TILE, (j + 1) * TILE)
+            for part, total in ((3, d_keys[j]), (1, d_values[j])):
+                total = total.astype(bf16).astype(f32)
+                d_hidden[at, lanes(part, h)] = (total * slope[at, lanes(part, h)]).astype(bf16)
+        return carry
+
+    lax.fori_loop(0, HEADS, attend_back, 0)
+
+    turned[...] = normed[...].T
+
+    def weight_step(r, carry):
+        at = tile(r)
+        for i in range(4):
+            cut = slice(i * width, (i + 1) * width)
+            grads[pl.ds(pl.multiple_of(i * width + r * TILE, TILE), TILE), :] = nn(
+                turned[at, :], d_hidden[:, cut]
+            ).astype(bf16)
+        d_normed = nt(d_hidden[at, :], w_in[...]).astype(bf16).astype(f32)
+        x = inputs[at, :].astype(f32)
+        normal = (x - jnp.mean(x, axis=-1, keepdims=True)) * scale[at, :]
+        d = norm_back(d_normed, normal, scale[at, :])
+        d_inputs[at, :] = (d + cotangent[at, :].astype(f32)).astype(bf16)
+        return carry
+
+    lax.fori_loop(0, steps, weight_step, 0)
+    turned[...] = gated[...].T
+
+    def last_step(r, carry):
+        at = tile(r)
+        grads[pl.ds(pl.multiple_of(4 * width + r * TILE, TILE), TILE), :] = nn(
+            turned[at, :], cotangent[...]
+        ).astype(bf16)
+        d_rows = nn(pick[at, :], d_inputs[...])
+        for k in range(4):
+            flat[pl.ds(r * 4 * TILE + k, TILE, stride=4), :] = d_rows[:, k * 128 : (k + 1) * 128]
+        return carry
+
+    lax.fori_loop(0, steps, last_step, 0)
+    grads[5 * width : 5 * width + onehot.shape[0], :] = nn(onehot[...], d_inputs[...]).astype(bf16)
+    grads[5 * width + onehot.shape[0] :, :] = jnp.zeros(
+        (grads.shape[0] - 5 * width - onehot.shape[0], width), bf16
+    )
+    back[...] = flat[...].astype(bf16).reshape(back.shape)
+
+
+def layer(lengths, slots, leaves, arrived, leaf_table, w_in, w_out, cotangent):
+    f32, bf16 = jnp.float32, jnp.bfloat16
+    count, width = cotangent.shape
+    vmem = pl.BlockSpec(memory_space=pltpu.VMEM)
+    smem = pl.BlockSpec(memory_space=pltpu.SMEM)
+    return pl.pallas_call(
+        layer_kernel,
+        out_shape=(
+            jax.ShapeDtypeStruct((count, width), bf16),
+            jax.ShapeDtypeStruct((ROWS_ALL, width), bf16),
+            jax.ShapeDtypeStruct(arrived.shape, bf16),
+        ),
+        in_specs=[smem] + [vmem] * 7,
+        out_specs=(vmem,) * 3,
+        scratch_shapes=[
+            pltpu.VMEM((count, count), bf16),
+            pltpu.VMEM((leaf_table.shape[0], count), bf16),
+            pltpu.VMEM((4 * count, 128), f32),
+            pltpu.VMEM((count, width), bf16),
+            pltpu.VMEM((count, width), bf16),
+            pltpu.VMEM((count, width), bf16),
+            pltpu.VMEM((count, 1), f32),
+            pltpu.VMEM((count, 4 * width), bf16),
+            pltpu.VMEM((count, 4 * width), f32),
+            pltpu.VMEM((HEADS, count, 3 * TILE), bf16),
+            pltpu.VMEM((HEADS, count, 3 * TILE), f32),
+            pltpu.VMEM((count, width), f32),
+            pltpu.VMEM((count, width), bf16),
+            pltpu.VMEM((count, width), bf16),
+            pltpu.VMEM((count, 4 * width), bf16),
+            pltpu.VMEM((width, count), bf16),
+            pltpu.VMEM((count, width), bf16),
+        ],
+    )(lengths, slots, leaves, arrived, leaf_table, w_in, w_out, cotangent)
+
+
 def on_device(
     item_table, requests, event_slot, lengths, leaf_ids, leaf_table, w_in, w_out, cotangent
 ):
-    width = item_table.shape[1]
     count = requests.shape[1]
     asks = jnp.pad(requests.reshape(count, 1, 2), ((0, 0), (0, 0), (0, BLOCK - 2)))
     blocks, asked = fetch_rows(asks, item_table)
-    arrived = blocks.reshape(-1, width)
-
-    def local_front(rows, table_leaf, weight_in):
-        return front(rows, event_slot, lengths[0], leaf_ids, table_leaf, weight_in)
-
-    (inputs, gated), pull_front = jax.vjp(local_front, arrived, leaf_table, w_in)
-    output, pull_back = jax.vjp(back, inputs, gated, w_out)
-    d_inputs, d_gated, d_out = pull_back(cotangent)
-    d_rows, d_leaf, d_in = pull_front((d_inputs, d_gated))
-    stacked = jnp.concatenate(
-        [d_in[:, i * width : (i + 1) * width] for i in range(4)]
-        + [d_out, d_leaf, jnp.zeros((ROWS_ALL - 2816, width), jnp.bfloat16)]
+    output, grads, d_blocks = layer(
+        lengths,
+        event_slot.reshape(1, -1),
+        leaf_ids.T,
+        blocks,
+        leaf_table,
+        w_in,
+        w_out,
+        cotangent,
     )
-    sums, returned = sum_all(stacked, d_rows.reshape(blocks.shape))
+    sums, returned = sum_all(grads, d_blocks)
     return (output, *finish(sums, returned, asked))
 
 

time: 203 us -> 154 us (0.76)
  matrix products: 34.7 us -> 0 us
  local copies, waits for them, and re-layouts: 30.1 us -> 1.56 us
  Pallas kernels: 125 us -> 152 us
  other arithmetic: 11.2 us -> 0 us
    dot_general x16 -> x0, matrix products: 34.7 us -> none  [the longest x3 9.3 us: front(): jnp.einsum('qhd,khd->hqk', query_heads, key_heads, preferred_element_type...]
    pallas_call x0 -> x1, Pallas kernels: none -> 26.7 us  [layer(): pl.pallas_call(layer_kernel, out_shape=(jax.ShapeDtypeStruct((count, widt...]
    reshape x9 -> x0, local copies, waits for them, and re-layouts: 16.7 us -> none  [the longest x2 4.75 us: front(): mixed = jnp.einsum('hqk,khd->qhd', weights, value_heads, preferred_elemen...]
    unnamed x38 -> x1, local copies, waits for them, and re-layouts: 11.9 us -> 0.81 us
    add_any x3 -> x0, other arithmetic: 5.96 us -> none  [the longest x1 3.47 us: front(): jax.nn.silu(jnp.dot(normed, w_in, preferred_element_type=jnp.float32))]
    reduce_sum x5 -> x0, other arithmetic: 3.96 us -> none  [the longest x2 2.94 us: normalize(): center = values - jnp.mean(values, axis=-1, keepdims=True)]
where the time goes in v3:
time: 154 us
  Pallas kernels  152 us (99%)
  local copies, waits for them, and re-layouts  1.56 us (1%)
    pallas_call x1, Pallas kernels, sum_all(): pl.pallas_call(sum_kernel, out_shape=(jax.ShapeDtypeStruct((ROWS_ALL, 512...  71.1 us
    pallas_call x1, Pallas kernels, fetch_rows(): pl.pallas_call(fetch_kernel, out_shape=(jax.ShapeDtypeStruct((count, 8, B...  45 us
    pallas_call x1, Pallas kernels, layer(): pl.pallas_call(layer_kernel, out_shape=(jax.ShapeDtypeStruct((count, widt...  26.7 us
    pallas_call x1, Pallas kernels, finish(): pl.pallas_call(finish_kernel, out_shape=(jax.ShapeDtypeStruct((128, 512),...  8.74 us

profile of v3, /device:TPU:1, one launch (start us, length us, event | category | flops | bytes accessed | tf_op | source)
XLA Modules:
  0.0 153.8 jit_solution(5107578423303643691)
XLA Ops:
  0.6 0.8 copy.14
  1.4 0.8 pad.4.req
  2.2 45.0 %shard_map.128 = (bf16[256,8,128]{2,1,0:T(8,128)(2,1)}, s32[256,1,128]{2,1,0:T(1,128)}) custom-call(s32[256,1,128]{2,1,0:T(1,128)} %pad.4.req, bf16[128,512]{1,0:T(8,128)(2,1)} %table.1), custom_call_target="tpu_custom_call" | custom-call | tf_op jit(solution)/shard_map/pallas_call | solution.py:145
  47.2 26.7 %shard_map.129 = (bf16[512,512]{1,0:T(8,128)(2,1)}, bf16[3072,512]{1,0:T(8,128)(2,1)}, bf16[256,8,128]{2,1,0:T(8,128)(2,1)}) custom-call(s32[1,4]{1,0:T(1,128)} %lengths.1, s32[1,512]{1,0:T(1,128)} %bitcast.5, s32[8,512]{1,0:T(8,128)} %bitcast.4, bf16[256,8,128]{2,1,0:T(8,128)(2,1)} %get-tuple-element.16.arrived, bf16[256,512]{1,0:T(8,128)(2,1)} %leaf_table.1, ...), custom_call_target="tpu_custom_call" | custom-call | tf_op jit(solution)/shard_map/pallas_call | solution.py:626
  73.9 71.1 %shard_map.130 = (bf16[3072,512]{1,0:T(8,128)(2,1)}, bf16[256,8,128]{2,1,0:T(8,128)(2,1)}) custom-call(bf16[3072,512]{1,0:T(8,128)(2,1)} %get-tuple-element.18.g, bf16[256,8,128]{2,1,0:T(8,128)(2,1)} %get-tuple-element.19.back), custom_call_target="tpu_custom_call" | custom-call | tf_op jit(solution)/shard_map/pallas_call | solution.py:400
  145.1 8.7 %shard_map.131 = (f32[128,512]{1,0:T(8,128)}, f32[256,512]{1,0:T(8,128)}, f32[512,2048]{1,0:T(8,128)}, f32[512,512]{1,0:T(8,128)}) custom-call(bf16[3072,512]{1,0:T(8,128)(2,1)} %get-tuple-element.20.sums, bf16[256,8,128]{2,1,0:T(8,128)(2,1)} %get-tuple-element.21.returned, s32[256,1,128]{2,1,0:T(1,128)} %get-tuple-element.22.asked), custom_call_target="tpu_custom_call" | custom-call | tf_op jit(solution)/shard_map/pallas_call | solution.py:200
